TPU v7x, 32 devices: a whole 2x2x4 slice. The times are simulated.
32 devices in a mesh: beam: 2 (over x), wide: 16 (over z, y, core).
Axes of the slice: x: 2, y: 2, z: 4, core: 2. Of those that a mesh axis runs over, the one named last changes fastest.
Arguments:
- filterbank: bfloat16 [2, 4096, 4096], P('beam', 'wide'), parts along dimension 0, may hold values from -100 to 100
- channel_mask: int32 [8192], P(('beam', 'wide')), parts along dimension 0, may hold values 0 or 1
- band_edges: int32 [7], replicated, may hold values from 385 to 3711, as said below
- dm_delays: int32 [16], replicated, may hold values from 0 to 2047
Outputs:
- series: float32 [2, 16, 4096], P('beam', 'wide'), parts along dimension 0
There are 2 independent parts, one for each index of `beam`. A program takes and returns all parts, laid end to end along the dimension named above; an argument that names none is the same for every part. Nothing has to cross between parts.
Inputs may be any that keep to these rules, and one draw needn't show every extreme that they name: `band_edges`: strictly increasing; entry i lies at (i + 1) * 512 up to a shift of less than 128.
All inputs are finite; a program needn't handle non-finite values. No bound on the sum of `channel_mask` on one device may be relied on, other than what follows from the above.
Results may differ from a plain program's by a relative error of at most 0.0063.
Values may be sent and summed in bfloat16 or wider, within the bound.
A program may use at most 64 MiB of HBM per device.

v0:
```python
import math

import jax
import jax.numpy as jnp
from jax import lax
from jax.sharding import PartitionSpec as P

C = 4096
NBLK = 8


def delay_fractions(channel_count, total_channels):
    channel_ids = jnp.arange(channel_count, dtype=jnp.int32)
    ratio = 0.5 + 0.5 * (channel_ids.astype(jnp.float32) + 0.5) / total_channels
    return (1.0 / (ratio * ratio) - 1.0) / 3.0


def noise_floors(band_power, band_edges, channels):
    bounds = jnp.concatenate(
        [jnp.zeros((1,), jnp.int32), band_edges, jnp.full((1,), channels, jnp.int32)]
    )
    widths = (bounds[1:] - bounds[:-1]).astype(jnp.float32)
    return jnp.sqrt(band_power / widths[None, :, None] + 1e-05)


def forward_tables(first_bin, bin_count, samples):
    bin_ids = first_bin + jnp.arange(bin_count, dtype=jnp.int32)
    times = jnp.arange(samples, dtype=jnp.int32)
    product = bin_ids[:, None] * times[None, :] % samples
    angle = product.astype(jnp.float32) * (2.0 * math.pi / samples)
    tables = jnp.stack([jnp.cos(angle), -jnp.sin(angle)], axis=0)
    return tables.reshape(2 * bin_count, samples).astype(jnp.bfloat16)


def inverse_tables(first_bin, bin_count, samples, channels):
    bin_ids = first_bin + jnp.arange(bin_count, dtype=jnp.int32)
    times = jnp.arange(samples, dtype=jnp.int32)
    product = bin_ids[:, None] * times[None, :] % samples
    angle = product.astype(jnp.float32) * (2.0 * math.pi / samples)
    weight = jnp.where(bin_ids == 0, 1.0, 2.0).astype(jnp.float32) / (samples * math.sqrt(channels))
    tables = jnp.stack(
        [weight[:, None] * jnp.cos(angle), -weight[:, None] * jnp.sin(angle)], axis=1
    )
    return tables.reshape(2 * bin_count, samples).astype(jnp.bfloat16)


def phase_tables(first_bin, bin_count, fractions, dm_delays, samples):
    bin_ids = first_bin + jnp.arange(bin_count, dtype=jnp.int32)
    cycles = (bin_ids[:, None] * dm_delays[None, :]).astype(jnp.float32)
    angle = cycles[:, None, :] * fractions[None, :, None] * (2.0 * math.pi / samples)
    return (jnp.cos(angle).astype(jnp.bfloat16), jnp.sin(angle).astype(jnp.bfloat16))


def spectrum_block(rows_flat, first_bin, bin_count, samples):
    tables = forward_tables(first_bin, bin_count, samples)
    block = lax.dot_general(
        tables, rows_flat, (((1,), (1,)), ((), ())), preferred_element_type=jnp.float32
    )
    return block.astype(jnp.bfloat16)


def dedisperse_block(spec_real, spec_imag, cos_tab, sin_tab):
    real_part = jnp.einsum(
        "fbc,fcd->fbd", spec_real, cos_tab, preferred_element_type=jnp.float32
    ) - jnp.einsum("fbc,fcd->fbd", spec_imag, sin_tab, preferred_element_type=jnp.float32)
    imag_part = jnp.einsum(
        "fbc,fcd->fbd", spec_real, sin_tab, preferred_element_type=jnp.float32
    ) + jnp.einsum("fbc,fcd->fbd", spec_imag, cos_tab, preferred_element_type=jnp.float32)
    return jnp.stack([real_part, imag_part], axis=1)


def body(filterbank, channel_mask, band_edges, dm_delays):
    beams, local_channels, samples = filterbank.shape
    group_size = lax.axis_size("wide")
    position = lax.axis_index("wide")
    first_channel = position * local_channels
    bands = band_edges.shape[0] + 1
    signal = filterbank.astype(jnp.float32).reshape(beams, local_channels, NBLK, samples // NBLK)
    power = jnp.mean(signal * signal, axis=3)
    channel_ids = first_channel + jnp.arange(local_channels, dtype=jnp.int32)
    band_ids = jnp.sum((band_edges[None, :] <= channel_ids[:, None]).astype(jnp.int32), axis=1)
    member = (band_ids[:, None] == jnp.arange(bands, dtype=jnp.int32)[None, :]).astype(jnp.float32)
    keep = channel_mask.astype(jnp.float32)
    local_power = jnp.einsum(
        "cj,bck->bjk", member * keep[:, None], power, precision=lax.Precision.HIGHEST
    )
    band_power = lax.psum(local_power, "wide")
    floors = noise_floors(band_power, band_edges, C)
    channel_floor = jnp.einsum("cj,bjk->bck", member, floors, precision=lax.Precision.HIGHEST)
    cleaned = (
        (signal / channel_floor[..., None] * keep[None, :, None, None])
        .reshape(beams, local_channels, samples)
        .astype(jnp.bfloat16)
    )
    rows_flat = cleaned.reshape(beams * local_channels, samples)
    bins = samples // 4
    local_bins = bins // group_size
    total_dms = dm_delays.shape[0]
    local_dms = total_dms // group_size
    dft_step = math.gcd(bins, 512)

    def fill_spectrum(step, buffer):
        first_bin = step * dft_step
        block = spectrum_block(rows_flat, first_bin, dft_step, samples).reshape(
            2, dft_step, beams, local_channels
        )
        return lax.dynamic_update_slice_in_dim(buffer, block, first_bin, 1)

    spectrum = lax.fori_loop(
        0,
        bins // dft_step,
        fill_spectrum,
        jnp.zeros((2, bins, beams, local_channels), jnp.bfloat16),
    )
    regrouped = lax.all_to_all(spectrum, "wide", split_axis=1, concat_axis=3, tiled=True)
    all_channels = regrouped.shape[3]
    fractions = delay_fractions(all_channels, all_channels)
    phase_step = math.gcd(local_bins, min(512, max(1, 2097152 // (all_channels * total_dms))))

    def fill_trials(step, buffer):
        offset = step * phase_step
        spec_part = lax.dynamic_slice_in_dim(regrouped, offset, phase_step, 1)
        cos_tab, sin_tab = phase_tables(
            position * local_bins + offset, phase_step, fractions, dm_delays, samples
        )
        block = dedisperse_block(spec_part[0], spec_part[1], cos_tab, sin_tab).astype(jnp.bfloat16)
        return lax.dynamic_update_slice_in_dim(buffer, block, offset, 0)

    dm_spectrum = lax.fori_loop(
        0,
        local_bins // phase_step,
        fill_trials,
        jnp.zeros((local_bins, 2, beams, total_dms), jnp.bfloat16),
    )
    by_trial = lax.all_to_all(dm_spectrum, "wide", split_axis=3, concat_axis=0, tiled=True)
    flat = by_trial.reshape(bins * 2, beams * local_dms)
    inverse_step = math.gcd(bins, 512)

    def add_series(step, total):
        first_bin = step * inverse_step
        part_rows = lax.dynamic_slice_in_dim(flat, first_bin * 2, inverse_step * 2, 0)
        table = inverse_tables(first_bin, inverse_step, samples, C)
        return total + lax.dot_general(
            part_rows, table, (((0,), (0,)), ((), ())), preferred_element_type=jnp.float32
        )

    series = lax.fori_loop(
        0, bins // inverse_step, add_series, jnp.zeros((beams * local_dms, samples), jnp.float32)
    )
    return series.reshape(beams, local_dms, samples)


def solution(mesh):
    return jax.shard_map(
        body,
        mesh=mesh,
        in_specs=(P("beam", "wide", None), P(("beam", "wide")), P(), P()),
        out_specs=P("beam", "wide", None),
        check_vma=False,
    )
```

profile of v0, /device:TPU:0, one launch (start us, length us, event | category | flops | bytes accessed | tf_op | source)
XLA Modules:
  0.0 588.3 jit_solution(12645496594164562645)
XLA Ops:
  0.0 0.7 convert_element_type.159
  0.7 2.1 convert_multiply_fusion
  2.8 5.7 copy.73
  8.5 0.1 convert_reduce_fusion
  8.6 2.7 reduce_sum.18
  11.3 0.4 convolution_bitcast_fusion.1
  11.7 35.2 %psum.7 = f32[1,8,8]{1,2,0:T(8,128)S(1)} all-reduce(f32[1,8,8]{1,2,0:T(8,128)S(1)} %convolution_bitcast_fusion.1), channel_id=1, replica_groups=mesh['beam'=2,'wide'=16] {'wide'}, use_global_device_ids=true, to_apply=%region_2.0 | all-reduce | flops 64 | bytes 512 | tf_op jit(solution)/shard_map/psum | solution.py:87
  47.0 0.1 fusion.61
  47.1 0.2 convolution_bitcast_fusion
  47.3 0.2 copy.55
  47.5 2.3 div.55
  49.8 4.9 div.56
  54.7 4.3 fusion.47
  59.1 1.5 broadcast_in_dim.59.clone
  60.6 97.5 %while.47 = (s32[]{:T(128)}, bf16[2,1024,1,256]{3,0,2,1:T(2,128)(2,1)}, bf16[256,4096]{1,0:T(8,128)(2,1)}, s32[]{:T(128)}, s32[]{:T(128)}, /*index=5*/s32[]{:T(128)}, s32[]{:T(128)}) while((s32[]{:T(128)}, bf16[2,1024,1,256]{3,0,2,1:T(2,128)(2,1)}, bf16[256,4096]{1,0:T(8,128)(2,1)}, s32[]{:T(128)}, s32[]{:T(128)}, /*index=5*/s32[]{:T(128)}, ...), condition=%wide.region_4.5_spmd, body=%wide.region_3.4_spmd.sunk | while | flops 2187592192 | bytes 45617308 | solution.py:109
  60.6 35.3 %cosine_convert_fusion.7 = (bf16[1,512,4096]{2,1,0:T(8,128)(2,1)S(1)}, bf16[1,512,4096]{2,1,0:T(8,128)(2,1)}) fusion(s32[512]{0:T(512)S(1)} %iota_add_fusion.7), kind=kLoop, calls=%fused_computation.9.clone.1 | loop fusion | flops 35651584 | bytes 8390656 | tf_op jit(solution)/shard_map/convert
  95.9 6.3 %pad_maximum_fusion.6 = bf16[2,512,4096]{2,1,0:T(8,128)(2,1)} fusion(bf16[1,512,4096]{2,1,0:T(8,128)(2,1)} %get-tuple-element.498, bf16[1,512,4096]{2,1,0:T(8,128)(2,1)S(1)} %get-tuple-element.499), kind=kLoop, calls=%fused_computation.7.clone.1 | loop fusion | flops 4194304 | bytes 16777216 | tf_op jit(solution)/shard_map/while/body/eval_jaxpr/stack | solution.py:31
  102.3 5.7 convolution_convert_fusion.2
  108.0 1.4 copy_dynamic-update-slice_fusion.2
  109.4 35.2 %cosine_convert_fusion.7 = (bf16[1,512,4096]{2,1,0:T(8,128)(2,1)S(1)}, bf16[1,512,4096]{2,1,0:T(8,128)(2,1)}) fusion(s32[512]{0:T(512)S(1)} %iota_add_fusion.7), kind=kLoop, calls=%fused_computation.9.clone.1 | loop fusion | flops 35651584 | bytes 8390656 | tf_op jit(solution)/shard_map/convert
  144.6 6.3 %pad_maximum_fusion.6 = bf16[2,512,4096]{2,1,0:T(8,128)(2,1)} fusion(bf16[1,512,4096]{2,1,0:T(8,128)(2,1)} %get-tuple-element.498, bf16[1,512,4096]{2,1,0:T(8,128)(2,1)S(1)} %get-tuple-element.499), kind=kLoop, calls=%fused_computation.7.clone.1 | loop fusion | flops 4194304 | bytes 16777216 | tf_op jit(solution)/shard_map/while/body/eval_jaxpr/stack | solution.py:31
  150.9 5.7 convolution_convert_fusion.2
  156.7 1.3 copy_dynamic-update-slice_fusion.2
  158.0 3.7 all-to-all-start
  161.7 22.9 %all-to-all-done = bf16[2,1024,1,256]{3,0,2,1:T(2,128)(2,1)S(1)} async-done(((bf16[2,1024,1,256]{3,0,2,1:T(2,128)(2,1)}), bf16[2,1024,1,256]{3,0,2,1:T(2,128)(2,1)S(1)}, u32[]{:S(2)}, u32[]{:S(2)}) %all-to-all-start) | async-done | bytes 1048608 | tf_op jit(solution)/shard_map/all_to_all | solution.py:115
  184.6 0.6 copy.84
  185.1 0.5 all_to_all.27
  185.7 0.6 broadcast_in_dim.58.clone
  186.3 235.6 %while.48 = (s32[]{:T(128)}, bf16[64,2,1,16]{0,1,2,3:T(2,128)(2,1)}, bf16[2,64,1,4096]{3,1,2,0:T(8,128)(2,1)S(1)}, s32[]{:T(128)}, s32[16]{0:T(128)S(1)}, /*inde...) while((s32[]{:T(128)}, bf16[64,2,1,16]{0,1,2,3:T(2,128)(2,1)}, ...), condition=%wide.region_6.7_spmd.clone, body=%wide.region_5.6_spmd.clone.sunk | while | flops 41979944 | bytes 2236923 | solution.py:129
  186.9 0.1 multiply_convert_fusion.5
  187.0 27.7 %fusion.88 = f32[32,1,16]{2,1,0:T(1,128)S(1)} fusion(f32[4096]{0:T(1024)S(1)} %add_multiply_fusion.2, f32[32,16]{1,0:T(8,128)S(1)} %multiply_convert_fusion.5, bf16[32,4096,1]{1,0,2:T(8,128)(2,1)S(1)} %get-tuple-element.506), kind=kOutput, calls=%fused_computation.20.clone.1 | convolution fusion | flops 10485760 | bytes 282624 | tf_op jit(solution)/shard_map/while/body/eval_jaxpr/fbc,fcd->fbd/dot_general | solution.py:63
  214.7 0.1 copy.102
  214.7 27.8 %fusion.89 = f32[32,1,16]{2,1,0:T(1,128)S(1)} fusion(f32[4096]{0:T(1024)S(1)} %add_multiply_fusion.2, f32[32,16]{1,0:T(8,128)S(1)} %multiply_convert_fusion.5, bf16[32,4096,1]{1,0,2:T(8,128)(2,1)S(1)} %get-tuple-element.505), kind=kOutput, calls=%fused_computation.19.clone.1 | convolution fusion | flops 10485760 | bytes 282624 | tf_op jit(solution)/shard_map/while/body/eval_jaxpr/fbc,fcd->fbd/dot_general | solution.py:68
  242.6 0.1 copy.103
  242.6 28.4 %fusion.90 = f32[32,1,16]{2,1,0:T(1,128)S(1)} fusion(f32[4096]{0:T(1024)S(1)} %add_multiply_fusion.2, f32[32,16]{1,0:T(8,128)S(1)} %multiply_convert_fusion.5, bf16[32,4096,1]{1,0,2:T(8,128)(2,1)S(1)} %get-tuple-element.506), kind=kOutput, calls=%fused_computation.21.clone.1 | convolution fusion | flops 10485760 | bytes 282624 | tf_op jit(solution)/shard_map/while/body/eval_jaxpr/fbc,fcd->fbd/dot_general | solution.py:66
  271.0 0.1 copy.104
  271.1 28.2 %fusion.87 = f32[32,1,16]{2,1,0:T(1,128)S(1)} fusion(f32[4096]{0:T(1024)S(1)} %add_multiply_fusion.2, f32[32,16]{1,0:T(8,128)S(1)} %multiply_convert_fusion.5, bf16[32,4096,1]{1,0,2:T(8,128)(2,1)S(1)} %get-tuple-element.505), kind=kOutput, calls=%fused_computation.22.clone.1 | convolution fusion | flops 10485760 | bytes 282624 | tf_op jit(solution)/shard_map/while/body/eval_jaxpr/fbc,fcd->fbd/dot_general | solution.py:65
  299.3 0.1 copy.101
  299.4 1.4 dynamic_update_slice.24
  301.3 0.1 multiply_convert_fusion.5
  301.4 27.7 %fusion.88 = f32[32,1,16]{2,1,0:T(1,128)S(1)} fusion(f32[4096]{0:T(1024)S(1)} %add_multiply_fusion.2, f32[32,16]{1,0:T(8,128)S(1)} %multiply_convert_fusion.5, bf16[32,4096,1]{1,0,2:T(8,128)(2,1)S(1)} %get-tuple-element.506), kind=kOutput, calls=%fused_computation.20.clone.1 | convolution fusion | flops 10485760 | bytes 282624 | tf_op jit(solution)/shard_map/while/body/eval_jaxpr/fbc,fcd->fbd/dot_general | solution.py:63
  329.0 0.1 copy.102
  329.1 27.8 %fusion.89 = f32[32,1,16]{2,1,0:T(1,128)S(1)} fusion(f32[4096]{0:T(1024)S(1)} %add_multiply_fusion.2, f32[32,16]{1,0:T(8,128)S(1)} %multiply_convert_fusion.5, bf16[32,4096,1]{1,0,2:T(8,128)(2,1)S(1)} %get-tuple-element.505), kind=kOutput, calls=%fused_computation.19.clone.1 | convolution fusion | flops 10485760 | bytes 282624 | tf_op jit(solution)/shard_map/while/body/eval_jaxpr/fbc,fcd->fbd/dot_general | solution.py:68
  356.9 0.1 copy.103
  357.0 28.4 %fusion.90 = f32[32,1,16]{2,1,0:T(1,128)S(1)} fusion(f32[4096]{0:T(1024)S(1)} %add_multiply_fusion.2, f32[32,16]{1,0:T(8,128)S(1)} %multiply_convert_fusion.5, bf16[32,4096,1]{1,0,2:T(8,128)(2,1)S(1)} %get-tuple-element.506), kind=kOutput, calls=%fused_computation.21.clone.1 | convolution fusion | flops 10485760 | bytes 282624 | tf_op jit(solution)/shard_map/while/body/eval_jaxpr/fbc,fcd->fbd/dot_general | solution.py:66
  385.4 0.1 copy.104
  385.4 28.2 %fusion.87 = f32[32,1,16]{2,1,0:T(1,128)S(1)} fusion(f32[4096]{0:T(1024)S(1)} %add_multiply_fusion.2, f32[32,16]{1,0:T(8,128)S(1)} %multiply_convert_fusion.5, bf16[32,4096,1]{1,0,2:T(8,128)(2,1)S(1)} %get-tuple-element.505), kind=kOutput, calls=%fused_computation.22.clone.1 | convolution fusion | flops 10485760 | bytes 282624 | tf_op jit(solution)/shard_map/while/body/eval_jaxpr/fbc,fcd->fbd/dot_general | solution.py:65
  413.7 3.1 dynamic_update_slice.24
  421.9 6.8 %all-to-all-start.1 = ((bf16[64,2,1,16]{0,1,2,3:T(2,128)(2,1)}), bf16[64,2,1,16]{0,1,2,3:T(2,128)(2,1)S(1)}, u32[]{:S(2)}, u32[]{:S(2)}) async-start(bf16[64,2,1,16]{0,1,2,3:T(2,128)(2,1)} %get-tuple-element.334), calls=%async_computation.1 | async-start | bytes 16384 | tf_op jit(solution)/shard_map/all_to_all | solution.py:135
  428.7 6.3 %all-to-all-done.1 = bf16[64,2,1,16]{0,1,2,3:T(2,128)(2,1)S(1)} async-done(((bf16[64,2,1,16]{0,1,2,3:T(2,128)(2,1)}), bf16[64,2,1,16]{0,1,2,3:T(2,128)(2,1)S(1)}, u32[]{:S(2)}, u32[]{:S(2)}) %all-to-all-start.1) | async-done | bytes 4128 | tf_op jit(solution)/shard_map/all_to_all | solution.py:135
  435.0 0.2 copy.68
  435.3 0.3 reshape.489
  435.6 152.0 %while.49 = (s32[]{:T(128)}, f32[1,4096]{1,0:T(1,128)S(1)}, bf16[2048,1]{0,1:T(2,128)(2,1)S(1)}, s32[]{:T(128)}, s32[]{:T(128)}, /*index=5*/s32[]{:T(128)}, s32[]{:T(128)}, s32[]{:T(128)}) while((s32[]{:T(128)}, f32[1,4096]{1,0:T(1,128)S(1)}, bf16[2048,1]{0,1:T(2,128)(2,1)S(1)}, s32[]{:T(128)}, s32[]{:T(128)}, ...), condition=%wide.region_8.9_spmd.clone, body=%wide.region_7.8_spmd.clone.sunk | while | flops 50342912 | bytes 67158176 | solution.py:147
  435.6 35.7 %multiply_convert_fusion.6 = (bf16[512,1,4096]{2,0,1:T(8,128)(2,1)S(1)}, bf16[512,1,4096]{2,0,1:T(8,128)(2,1)}) fusion(s32[512]{0:T(512)S(1)} %iota_add_fusion.9, f32[512]{0:T(512)S(1)} %get-tuple-element.512, f32[512]{0:T(512)S(1)} %get-tuple-element.513), kind=kLoop, calls=%fused_computation.63.clone.1 | loop fusion | flops 37748736 | bytes 8394752 | tf_op jit(solution)/shard_map/convert.6
  471.3 6.2 %pad_maximum_fusion.8 = bf16[512,2,4096]{2,0,1:T(8,128)(2,1)} fusion(bf16[512,1,4096]{2,0,1:T(8,128)(2,1)} %get-tuple-element.514, bf16[512,1,4096]{2,0,1:T(8,128)(2,1)S(1)} %get-tuple-element.515), kind=kLoop, calls=%fused_computation.61.clone.1 | loop fusion | flops 4194304 | bytes 16777216 | tf_op jit(solution)/shard_map/while/body/eval_jaxpr/stack | solution.py:41
  477.4 16.4 %copy.106 = bf16[512,2,4096]{2,1,0:T(2,128)(2,1)} copy(bf16[512,2,4096]{2,0,1:T(8,128)(2,1)} %pad_maximum_fusion.8) | data formatting | bytes 16777216 | tf_op jit(solution)/shard_map/while/body/eval_jaxpr/stack | solution.py:41
  493.8 13.1 %convert_element_type.227 = bf16[1024,4096]{1,0:T(8,128)(2,1)} reshape(bf16[512,2,4096]{2,1,0:T(2,128)(2,1)} %copy.106) | data formatting | bytes 16777216 | tf_op jit(solution)/shard_map/while/body/eval_jaxpr/convert_element_type | solution.py:44
  507.0 4.6 convolution_add_fusion.2
  511.6 35.7 %multiply_convert_fusion.6 = (bf16[512,1,4096]{2,0,1:T(8,128)(2,1)S(1)}, bf16[512,1,4096]{2,0,1:T(8,128)(2,1)}) fusion(s32[512]{0:T(512)S(1)} %iota_add_fusion.9, f32[512]{0:T(512)S(1)} %get-tuple-element.512, f32[512]{0:T(512)S(1)} %get-tuple-element.513), kind=kLoop, calls=%fused_computation.63.clone.1 | loop fusion | flops 37748736 | bytes 8394752 | tf_op jit(solution)/shard_map/convert.6
  547.2 6.2 %pad_maximum_fusion.8 = bf16[512,2,4096]{2,0,1:T(8,128)(2,1)} fusion(bf16[512,1,4096]{2,0,1:T(8,128)(2,1)} %get-tuple-element.514, bf16[512,1,4096]{2,0,1:T(8,128)(2,1)S(1)} %get-tuple-element.515), kind=kLoop, calls=%fused_computation.61.clone.1 | loop fusion | flops 4194304 | bytes 16777216 | tf_op jit(solution)/shard_map/while/body/eval_jaxpr/stack | solution.py:41
  553.4 16.4 %copy.106 = bf16[512,2,4096]{2,1,0:T(2,128)(2,1)} copy(bf16[512,2,4096]{2,0,1:T(8,128)(2,1)} %pad_maximum_fusion.8) | data formatting | bytes 16777216 | tf_op jit(solution)/shard_map/while/body/eval_jaxpr/stack | solution.py:41
  569.8 13.1 %convert_element_type.227 = bf16[1024,4096]{1,0:T(8,128)(2,1)} reshape(bf16[512,2,4096]{2,1,0:T(2,128)(2,1)} %copy.106) | data formatting | bytes 16777216 | tf_op jit(solution)/shard_map/while/body/eval_jaxpr/convert_element_type | solution.py:44
  582.9 4.6 convolution_add_fusion.2
  587.5 0.6 copy-done.2
  (32 shorter events, 0.3 us)
Async XLA Ops:
  0.0 8.5 %copy-start.4 = (s32[7]{0:T(128)S(1)}, s32[7]{0:T(128)}, u32[]{:S(2)}) copy-start(s32[7]{0:T(128)} %param.12) | copy-start | bytes 88
  8.6 46.1 %copy-start = (bf16[1,256,4096]{2,1,0:T(8,128)(2,1)S(1)}, bf16[1,256,4096]{2,1,0:T(8,128)(2,1)}, u32[]{:S(2)}) copy-start(bf16[1,256,4096]{2,1,0:T(8,128)(2,1)} %param.10) | copy-start | bytes 6291460
  60.6 125.7 %copy-start.3 = (s32[16]{0:T(128)S(1)}, s32[16]{0:T(128)}, u32[]{:S(2)}) copy-start(s32[16]{0:T(128)} %param.13) | copy-start | bytes 196
  95.9 6.3 %copy-start.1 = (bf16[256,4096]{1,0:T(8,128)(2,1)S(1)}, bf16[256,4096]{1,0:T(8,128)(2,1)}, u32[]{:S(2)}) copy-start(bf16[256,4096]{1,0:T(8,128)(2,1)} %get-tuple-element.532) | copy-start | bytes 6291460 | tf_op jit(solution)/shard_map/while
  144.6 6.3 %copy-start.1 = (bf16[256,4096]{1,0:T(8,128)(2,1)S(1)}, bf16[256,4096]{1,0:T(8,128)(2,1)}, u32[]{:S(2)}) copy-start(bf16[256,4096]{1,0:T(8,128)(2,1)} %get-tuple-element.532) | copy-start | bytes 6291460 | tf_op jit(solution)/shard_map/while
  158.0 26.5 %all-to-all-start = ((bf16[2,1024,1,256]{3,0,2,1:T(2,128)(2,1)}), bf16[2,1024,1,256]{3,0,2,1:T(2,128)(2,1)S(1)}, u32[]{:S(2)}, u32[]{:S(2)}) async-start(bf16[2,1024,1,256]{3,0,2,1:T(2,128)(2,1)} %get-tuple-element.333), calls=%async_computation | async-start | bytes 2097152 | tf_op jit(solution)/shard_map/all_to_all | solution.py:115
  421.9 13.1 %all-to-all-start.1 = ((bf16[64,2,1,16]{0,1,2,3:T(2,128)(2,1)}), bf16[64,2,1,16]{0,1,2,3:T(2,128)(2,1)S(1)}, u32[]{:S(2)}, u32[]{:S(2)}) async-start(bf16[64,2,1,16]{0,1,2,3:T(2,128)(2,1)} %get-tuple-element.334), calls=%async_computation.1 | async-start | bytes 16384 | tf_op jit(solution)/shard_map/all_to_all | solution.py:135
  587.5 0.6 copy-start.2
where the time goes:
time: 594 us; the launch traced here: 588 us
  matrix products  245 us (41%)
  other arithmetic  177 us (30%)
  local copies, waits for them, and re-layouts  84.5 us (14%)
  blocking collectives  35.2 us (6%)
  waiting for transfers between devices  29.2 us (5%)
  starting transfers between devices  10.4 us (2%)
  loops' own time  6.19 us (1%)
    another operation x4, other arithmetic  142 us
    dot_general x2, matrix products, dedisperse_block(): jnp.einsum('fbc,fcd->fbd', spec_real, sin_tab, preferred_element_type=jnp...  56.8 us
    dot_general x2, matrix products, dedisperse_block(): jnp.einsum('fbc,fcd->fbd', spec_imag, sin_tab, preferred_element_type=jnp...  56.3 us
    dot_general x2, matrix products, dedisperse_block(): jnp.einsum('fbc,fcd->fbd', spec_imag, cos_tab, preferred_element_type=jnp...  55.6 us
    dot_general x2, matrix products, dedisperse_block(): jnp.einsum('fbc,fcd->fbd', spec_real, cos_tab, preferred_element_type=jnp...  55.3 us
    psum x1, blocking collectives, body(): band_power = lax.psum(local_power, 'wide')  35.2 us
    another operation x2, local copies, waits for them, and re-layouts, inverse_tables(): jnp.stack([weight[:, None] * jnp.cos(angle), -weight[:, None] * jnp.sin(a...  32.8 us
    convert_element_type x2, local copies, waits for them, and re-layouts, inverse_tables(): return tables.reshape(2 * bin_count, samples).astype(jnp.bfloat16)  26.3 us
  transfers between devices with their start and end apart: 2, of which 2 were waited for; matrix products, arithmetic and copies ran while one was open for 0% of the time, Pallas kernels for 0%

commit v1 on v0

v1 whole, which is shorter than its diff:
```python
import functools
import math

import jax
import jax.numpy as jnp
import numpy as np
from jax import lax
from jax.experimental import pallas as pl
from jax.experimental.pallas import tpu as pltpu
from jax.sharding import PartitionSpec as P

NBLK = 8
LANES = 128
VMEM = pl.BlockSpec(memory_space=pltpu.VMEM)
SMEM = pl.BlockSpec(memory_space=pltpu.SMEM)
MESH = pl.DeviceIdType.MESH
HIGH = lax.Precision.HIGHEST


def turn_coefficients():
    degree = 5
    nodes = np.cos((np.arange(64) + 0.5) * np.pi / 64) * 0.125 + 0.125
    root = np.sqrt(nodes)
    cos_fit = np.polynomial.Chebyshev.fit(nodes, np.cos(2 * np.pi * root), degree, domain=[0, 0.25])
    sin_fit = np.polynomial.Chebyshev.fit(
        nodes, np.sin(2 * np.pi * root) / root, degree, domain=[0, 0.25]
    )
    as_power = lambda fit: [float(np.float32(v)) for v in fit.convert(kind=np.polynomial.Polynomial).coef]
    return as_power(cos_fit), as_power(sin_fit)


COS_COEF, SIN_COEF = turn_coefficients()


def cos_sin_turns(turns):
    r = turns - jnp.floor(turns + 0.5)
    s = r * r
    c = jnp.full_like(s, COS_COEF[-1])
    q = jnp.full_like(s, SIN_COEF[-1])
    for a, b in zip(COS_COEF[-2::-1], SIN_COEF[-2::-1]):
        c = c * s + a
        q = q * s + b
    return c, q * r


def forward_seeds(samples):
    fine = 32
    quarter = samples // 4
    f = (4 * np.arange(quarter // 4)[None, :] + np.arange(4)[:, None]).reshape(-1)
    coarse = (np.arange(quarter // fine) * fine)[:, None] * f[None, :] % samples
    small = np.arange(fine)[:, None] * f[None, :] % samples
    out = []
    for product in (coarse, small):
        angle = product * (2 * np.pi / samples)
        out += [np.cos(angle), np.sin(angle)]
    return [v.astype(np.float32) for v in out]


def inverse_seeds(samples, channels):
    halves = samples // 16 // LANES
    lane = np.arange(LANES)
    r = np.repeat(np.arange(4), halves)
    h = np.tile(np.arange(halves), 4)
    f = 4 * LANES * h[:, None] + 4 * lane[None, :] + r[:, None]
    weight = np.where(f == 0, 1.0, 2.0) / (samples * math.sqrt(channels))
    angle = (f[:, :, None] * np.arange(LANES)[None, None, :] % samples) * (2 * np.pi / samples)
    first = [weight[:, :, None] * np.cos(angle), weight[:, :, None] * np.sin(angle)]
    steps = samples // LANES
    b = 4 * lane[None, :] + np.arange(4)[:, None]
    turn = (b[:, None, :] * np.arange(steps)[None, :, None] % steps) * (2 * np.pi / steps)
    second = [np.cos(turn), np.sin(turn)]
    return [v.astype(np.float32) for v in first + second]


def member_rows(edges_ref, channel, bands, channels):
    rows = []
    for j in range(bands):
        inside = channel < (channels if j == bands - 1 else edges_ref[j])
        if j:
            inside = jnp.logical_and(inside, channel >= edges_ref[j - 1])
        rows.append(inside)
    return rows


def power_kernel(bands, channels, edges_ref, mask_ref, x_ref, out_ref, acc_ref):
    local, samples = x_ref.shape
    window = samples // NBLK
    first = lax.axis_index("wide") * local
    rows = 64

    def square(i, carry):
        at = pl.ds(pl.multiple_of(i * rows, rows), rows)
        for k in range(NBLK):
            total = None
            for p in range(window // LANES):
                v = x_ref[at, pl.ds(k * window + p * LANES, LANES)].astype(jnp.float32)
                total = v * v if total is None else total + v * v
            acc_ref[at, pl.ds(k * LANES, LANES)] = total
        return carry

    lax.fori_loop(0, local // rows, square, 0)
    channel = first + lax.broadcasted_iota(jnp.int32, (1, local), 1)
    keep = mask_ref[...].astype(jnp.float32)
    picks = [jnp.where(m, keep, 0.0) for m in member_rows(edges_ref, channel, bands, channels)]
    pick = jnp.concatenate(picks, axis=0)
    summed = jnp.dot(pick, acc_ref[...], precision=HIGH, preferred_element_type=jnp.float32)
    lane = lax.broadcasted_iota(jnp.int32, (bands, LANES), 1)
    out = jnp.zeros((bands, LANES), jnp.float32)
    for k in range(NBLK):
        part = jnp.sum(summed[:, k * LANES : (k + 1) * LANES], axis=1, keepdims=True)
        out = jnp.where(lane == k, part / window, out)
    out_ref[...] = out


def share_kernel(n, x_ref, out_ref, got, send_sem, recv_sem):
    me = lax.axis_index("wide")
    barrier = pltpu.get_barrier_semaphore()
    for step in range(1, n):
        pl.semaphore_signal(
            barrier, inc=1, device_id={"wide": lax.rem(me + step, n)}, device_id_type=MESH
        )
    pl.semaphore_wait(barrier, n - 1)
    copies = []
    for step in range(1, n):
        copy = pltpu.make_async_remote_copy(
            src_ref=x_ref,
            dst_ref=got.at[step],
            send_sem=send_sem.at[step],
            recv_sem=recv_sem.at[step],
            device_id={"wide": lax.rem(me + step, n)},
            device_id_type=MESH,
        )
        copy.start()
        copies.append(copy)
    total = x_ref[...]
    for step in range(1, n):
        copies[step - 1].wait()
        total = total + got[step]
    out_ref[...] = total


def spectrum_kernel(
    bands, channels, trials,
    edges_ref, delays_ref, mask_ref, power_ref, x_ref, ac_ref, as_ref, bc_ref, bs_ref,
    out_ref,
    tab_cos, tab_sin, y_ref, spec_re, spec_im, rot_ref, frac_ref,
):
    local, samples = x_ref.shape
    quarter = samples // 4
    window = samples // NBLK
    group = quarter // 4
    halves = group // LANES
    first = lax.axis_index("wide") * local
    fine = bc_ref.shape[0]

    def fill(i, carry):
        at = pl.ds(pl.multiple_of(i * fine, fine), fine)
        ca, sa = ac_ref[pl.ds(i, 1), :], as_ref[pl.ds(i, 1), :]
        cb, sb = bc_ref[...], bs_ref[...]
        tab_cos[at, :] = (ca * cb - sa * sb).astype(jnp.bfloat16)
        tab_sin[at, :] = (sa * cb + ca * sb).astype(jnp.bfloat16)
        return carry

    lax.fori_loop(0, quarter // fine, fill, 0)

    channel = first + lax.broadcasted_iota(jnp.int32, (local, LANES), 0)
    ratio = 0.5 + 0.5 * (channel.astype(jnp.float32) + 0.5) / channels
    fraction = (1.0 / (ratio * ratio) - 1.0) / 3.0
    frac_ref[...] = fraction
    lane = lax.broadcasted_iota(jnp.int32, (1, LANES), 1)
    delay_row = jnp.zeros((1, LANES), jnp.float32)
    for d in range(trials):
        delay_row = jnp.where(lane == d, delays_ref[d].astype(jnp.float32), delay_row)
    sweep = fraction * (delay_row * (1.0 / samples))
    rotations = cos_sin_turns(sweep) + cos_sin_turns(sweep * (4.0 * LANES))
    for d in range(trials):
        for i, rot in enumerate(rotations):
            rot_ref[d, i] = jnp.broadcast_to(rot[:, d : d + 1], (local, LANES))

    scale = jnp.zeros((local, LANES), jnp.float32)
    members = member_rows(edges_ref, channel, bands, channels)
    for j in range(bands):
        high = channels if j == bands - 1 else edges_ref[j]
        low = edges_ref[j - 1] if j else 0
        width = jnp.full((1, LANES), high - low, jnp.int32).astype(jnp.float32)
        level = 1.0 / jnp.sqrt(power_ref[j : j + 1, :] / width + 1e-05)
        scale = jnp.where(members[j], level, scale)
    scale = scale * mask_ref[...].astype(jnp.float32)

    per = quarter // window
    for h in range(per):
        columns = [scale[:, m * per + h : m * per + h + 1] for m in range(4)]
        for p in range(window // LANES):
            start = h * window + p * LANES
            x0, x1, x2, x3 = (
                x_ref[:, m * quarter + start : m * quarter + start + LANES].astype(jnp.float32)
                * columns[m]
                for m in range(4)
            )
            here = slice(start, start + LANES)
            y_ref[0, :, here] = ((x0 + x2) + (x1 + x3)).astype(jnp.bfloat16)
            y_ref[1, :, here] = ((x0 + x2) - (x1 + x3)).astype(jnp.bfloat16)
            y_ref[2, :, here] = (x0 - x2).astype(jnp.bfloat16)
            y_ref[3, :, here] = (x1 - x3).astype(jnp.bfloat16)

    def product(which, table, r):
        return jnp.dot(
            y_ref[which], table[:, r * group : (r + 1) * group], preferred_element_type=jnp.float32
        )

    def put(r, real, imag):
        spec_re[:, r * group : (r + 1) * group] = real
        spec_im[:, r * group : (r + 1) * group] = imag

    put(0, product(0, tab_cos, 0), -product(0, tab_sin, 0))
    put(2, product(1, tab_cos, 2), -product(1, tab_sin, 2))
    put(1, product(2, tab_cos, 1) - product(3, tab_sin, 1),
        -(product(2, tab_sin, 1) + product(3, tab_cos, 1)))
    put(3, product(2, tab_cos, 3) + product(3, tab_sin, 3),
        product(3, tab_cos, 3) - product(2, tab_sin, 3))

    lane_step = lax.broadcasted_iota(jnp.int32, (8, LANES), 1).astype(jnp.float32) * 4.0
    blocks = 4 * halves

    def trial(d, carry):
        delay = delays_ref[d].astype(jnp.float32) * (1.0 / samples)
        per_lane = lane_step * delay

        def rotate(i, totals):
            at = pl.ds(pl.multiple_of(i * 8, 8), 8)
            base_re, base_im = cos_sin_turns(frac_ref[at, :] * per_lane)
            one_re, one_im = rot_ref[d, 0, at, :], rot_ref[d, 1, at, :]
            far_re, far_im = rot_ref[d, 2, at, :], rot_ref[d, 3, at, :]
            totals = list(totals)
            for h in range(halves):
                e_re, e_im = base_re, base_im
                for r in range(4):
                    col = pl.ds((r * halves + h) * LANES, LANES)
                    s_re, s_im = spec_re[at, col], spec_im[at, col]
                    k = r * halves + h
                    totals[k] = totals[k] + (s_re * e_re - s_im * e_im)
                    totals[blocks + k] = totals[blocks + k] + (s_re * e_im + s_im * e_re)
                    if r < 3:
                        e_re, e_im = e_re * one_re - e_im * one_im, e_re * one_im + e_im * one_re
                if h < halves - 1:
                    base_re, base_im = (
                        base_re * far_re - base_im * far_im,
                        base_re * far_im + base_im * far_re,
                    )
            return tuple(totals)

        zero = jnp.zeros((8, LANES), jnp.float32)
        totals = lax.fori_loop(0, local // 8, rotate, (zero,) * (2 * blocks))
        out_ref[d] = jnp.concatenate([jnp.sum(v, axis=0, keepdims=True) for v in totals], axis=0)
        return carry

    lax.fori_loop(0, trials, trial, 0)


def trade_kernel(n, x_ref, out_ref, got, send_sem, recv_sem):
    me = lax.axis_index("wide")
    share = out_ref.shape[0]
    barrier = pltpu.get_barrier_semaphore()
    for step in range(1, n):
        pl.semaphore_signal(
            barrier, inc=1, device_id={"wide": lax.rem(me + step, n)}, device_id_type=MESH
        )
    pl.semaphore_wait(barrier, n - 1)
    copies = []
    for step in range(1, n):
        to = lax.rem(me + step, n)
        copy = pltpu.make_async_remote_copy(
            src_ref=x_ref.at[pl.ds(to * share, share)],
            dst_ref=got.at[step],
            send_sem=send_sem.at[step],
            recv_sem=recv_sem.at[step],
            device_id={"wide": to},
            device_id_type=MESH,
        )
        copy.start()
        copies.append(copy)
    total = x_ref[pl.ds(me * share, share)]
    for step in range(1, n):
        copies[step - 1].wait()
        total = total + got[step]
    out_ref[...] = total


def series_kernel(x_ref, fc_ref, fs_ref, gc_ref, gs_ref, out_ref):
    blocks = fc_ref.shape[0]
    halves = blocks // 4
    for b in range(x_ref.shape[0]):
        rounded = x_ref[b].astype(jnp.bfloat16).astype(jnp.float32)
        turned = jnp.transpose(rounded)
        series = None
        for r in range(4):
            re = im = None
            for h in range(halves):
                k = r * halves + h
                d_re, d_im = turned[:, k : k + 1], turned[:, blocks + k : blocks + k + 1]
                p_re = d_re * fc_ref[k] - d_im * fs_ref[k]
                p_im = d_re * fs_ref[k] + d_im * fc_ref[k]
                re = p_re if re is None else re + p_re
                im = p_im if im is None else im + p_im
            part = jnp.dot(
                gc_ref[r], re, precision=HIGH, preferred_element_type=jnp.float32
            ) - jnp.dot(gs_ref[r], im, precision=HIGH, preferred_element_type=jnp.float32)
            series = part if series is None else series + part
        out_ref[b] = series


def exchange(kernel, n, x, out_shape, slot, collective_id):
    return pl.pallas_call(
        functools.partial(kernel, n),
        out_shape=jax.ShapeDtypeStruct(out_shape, x.dtype),
        in_specs=[VMEM],
        out_specs=VMEM,
        scratch_shapes=[
            pltpu.VMEM((n,) + slot, x.dtype),
            pltpu.SemaphoreType.DMA((n,)),
            pltpu.SemaphoreType.DMA((n,)),
        ],
        compiler_params=pltpu.CompilerParams(collective_id=collective_id, has_side_effects=True),
    )(x)


def body(n, filterbank, channel_mask, band_edges, dm_delays):
    beams, local, samples = filterbank.shape
    channels = local * n
    bands = band_edges.shape[0] + 1
    trials = dm_delays.shape[0]
    share = trials // n
    quarter = samples // 4
    blocks = quarter // LANES
    steps = samples // LANES
    ac, as_, bc, bs = forward_seeds(samples)
    fc, fs, gc, gs = inverse_seeds(samples, channels)
    x = filterbank.reshape(local, samples)

    local_power = pl.pallas_call(
        functools.partial(power_kernel, bands, channels),
        out_shape=jax.ShapeDtypeStruct((bands, LANES), jnp.float32),
        in_specs=[SMEM, VMEM, VMEM],
        out_specs=VMEM,
        scratch_shapes=[pltpu.VMEM((local, NBLK * LANES), jnp.float32)],
    )(band_edges, channel_mask.reshape(1, local), x)
    band_power = exchange(
        share_kernel, n, local_power, (bands, LANES), (bands, LANES), 0
    )
    partial = pl.pallas_call(
        functools.partial(spectrum_kernel, bands, channels, trials),
        out_shape=jax.ShapeDtypeStruct((trials, 2 * blocks, LANES), jnp.float32),
        in_specs=[SMEM, SMEM] + [VMEM] * 7,
        out_specs=VMEM,
        scratch_shapes=[
            pltpu.VMEM((quarter, quarter), jnp.bfloat16),
            pltpu.VMEM((quarter, quarter), jnp.bfloat16),
            pltpu.VMEM((4, local, quarter), jnp.bfloat16),
            pltpu.VMEM((local, quarter), jnp.float32),
            pltpu.VMEM((local, quarter), jnp.float32),
            pltpu.VMEM((trials, 4, local, LANES), jnp.float32),
            pltpu.VMEM((local, LANES), jnp.float32),
        ],
    )(band_edges, dm_delays, channel_mask.reshape(local, 1), band_power, x, ac, as_, bc, bs)
    summed = exchange(
        trade_kernel, n, partial, (share, 2 * blocks, LANES), (share, 2 * blocks, LANES), 1
    )
    series = pl.pallas_call(
        series_kernel,
        out_shape=jax.ShapeDtypeStruct((share, steps, LANES), jnp.float32),
        in_specs=[VMEM] * 5,
        out_specs=VMEM,
    )(summed, fc, fs, gc, gs)
    return series.reshape(beams, share, samples)


def solution(mesh):
    return jax.shard_map(
        functools.partial(body, mesh.shape["wide"]),
        mesh=mesh,
        in_specs=(P("beam", "wide", None), P(("beam", "wide")), P(), P()),
        out_specs=P("beam", "wide", None),
        check_vma=False,
    )
```

time: 594 us -> 54.6 us (0.09)
  matrix products: 245 us -> 0 us
  other arithmetic: 177 us -> 0 us
  local copies, waits for them, and re-layouts: 84.5 us -> 0.8 us
  Pallas kernels: 0 us -> 53.5 us
  blocking collectives: 35.2 us -> 0 us
  waiting for transfers between devices: 29.2 us -> 0 us
  starting transfers between devices: 10.4 us -> 0 us
  loops' own time: 6.19 us -> 0 us
    dot_general x14 -> x0, matrix products: 245 us -> none  [the longest x2 56.8 us: dedisperse_block(): jnp.einsum('fbc,fcd->fbd', spec_real, sin_tab, preferred_element_type=jnp...]
    another operation x12 -> x0, other arithmetic: 167 us -> none
    pallas_call x0 -> x5, Pallas kernels: none -> 53.5 us  [the longest x1 28.4 us: body(): pl.pallas_call(functools.partial(spectrum_kernel, bands, channels, trials...]
    psum x1 -> x0, blocking collectives: 35.2 us -> none  [body(): band_power = lax.psum(local_power, 'wide')]
    another operation x4 -> x0, local copies, waits for them, and re-layouts: 32.9 us -> none  [the longest x2 32.8 us: inverse_tables(): jnp.stack([weight[:, None] * jnp.cos(angle), -weight[:, None] * jnp.sin(a...]
    all_to_all x2 -> x0, waiting for transfers between devices: 29.2 us -> none  [the longest x1 22.9 us: body(): lax.all_to_all(spectrum, 'wide', split_axis=1, concat_axis=3, tiled=True)]
    convert_element_type x2 -> x0, local copies, waits for them, and re-layouts: 26.3 us -> none  [inverse_tables(): return tables.reshape(2 * bin_count, samples).astype(jnp.bfloat16)]
    all_to_all x2 -> x0, starting transfers between devices: 10.4 us -> none  [the longest x1 6.75 us: body(): lax.all_to_all(dm_spectrum, 'wide', split_axis=3, concat_axis=0, tiled=True)]
  transfers between devices with their start and end apart: 2 -> 0, of which waited for: 2 -> 0; matrix products, arithmetic and copies ran while one was open for 0% -> 0% of each run, Pallas kernels for 0% -> 0%
where the time goes in v1:
time: 54.6 us; the launch traced here: 54.4 us
  Pallas kernels  53.5 us (98%)
  local copies, waits for them, and re-layouts  0.8 us (1%)
    pallas_call x1, Pallas kernels, body(): pl.pallas_call(functools.partial(spectrum_kernel, bands, channels, trials...  28.4 us
    pallas_call x2, Pallas kernels, exchange(): pl.pallas_call(functools.partial(kernel, n), out_shape=jax.ShapeDtypeStru...  19.2 us
    pallas_call x1, Pallas kernels, body(): pl.pallas_call(functools.partial(power_kernel, bands, channels), out_shap...  3.29 us
    pallas_call x1, Pallas kernels, body(): pl.pallas_call(series_kernel, out_shape=jax.ShapeDtypeStruct((share, step...  2.61 us

profile of v1, /device:TPU:0, one launch (start us, length us, event | category | flops | bytes accessed | tf_op | source)
XLA Modules:
  0.0 54.4 jit_solution(12085077515781616724)
XLA Ops:
  0.0 0.0 copy-start
  0.0 3.3 %shard_map.118.x_ref = f32[8,128]{1,0:T(8,128)} custom-call(s32[7]{0:T(128)} %edges_ref.3, s32[1,256]{1,0:T(1,128)} %bitcast.6, bf16[256,4096]{1,0:T(8,128)(2,1)} %bitcast.4), custom_call_target="tpu_custom_call" | custom-call | tf_op jit(solution)/shard_map/pallas_call | solution.py:340
  3.3 10.2 %shard_map.119.power_ref = f32[8,128]{1,0:T(8,128)} custom-call(f32[8,128]{1,0:T(8,128)} %shard_map.118.x_ref), custom_call_target="tpu_custom_call" | custom-call | tf_op jit(solution)/shard_map/pallas_call | solution.py:313
  13.5 0.0 copy-done
  13.5 0.8 %copy.13.mask_ref = s32[256,1]{1,0:T(8,128)} copy(s32[256,1]{0,1:T(1,128)S(1)} %bitcast.7) | data formatting | bytes 2048 | tf_op jit(solution)/shard_map/reshape | solution.py:364
  14.3 28.4 %shard_map.120.x_ref = f32[16,16,128]{2,1,0:T(8,128)} custom-call(s32[7]{0:T(128)} %edges_ref.3, s32[16]{0:T(128)} %delays_ref.1, s32[256,1]{1,0:T(8,128)} %copy.13.mask_ref, f32[8,128]{1,0:T(8,128)} %shard_map.119.power_ref, bf16[256,4096]{1,0:T(8,128)(2,1)} %bitcast.5, f32[32,1024]{1,0:T(8,128)} %constant.16.clone.ac_ref, ...), custom_call_target="tpu_custom_call" | custom-call | tf_op jit(solution)/shard_map/pallas_call | solution.py:350
  42.7 9.0 %shard_map.121.x_ref = f32[1,16,128]{2,1,0:T(8,128)} custom-call(f32[16,16,128]{2,1,0:T(8,128)} %shard_map.120.x_ref), custom_call_target="tpu_custom_call" | custom-call | tf_op jit(solution)/shard_map/pallas_call | solution.py:313
  51.8 2.6 %shard_map.122 = f32[1,32,128]{2,1,0:T(8,128)} custom-call(f32[1,16,128]{2,1,0:T(8,128)} %shard_map.121.x_ref, f32[8,128,128]{2,1,0:T(8,128)} %constant.20.clone.fc_ref, f32[8,128,128]{2,1,0:T(8,128)} %constant.21.clone.fs_ref, f32[4,32,128]{2,1,0:T(8,128)} %constant.22.clone.gc_ref, f32[4,32,128]{2,1,0:T(8,128)} %constant.23.clone.gs_ref), custom_call_target="tpu_custom_call" | custom-call | tf_op jit(solution)/shard_map/pallas_call | solution.py:368
Async XLA Ops:
  0.0 13.5 %copy-start = (s32[256]{0:T(256)S(1)}, s32[256]{0:T(256)}, u32[]{:S(2)}) copy-start(s32[256]{0:T(256)} %param.13) | copy-start | bytes 3076

commit v2 on v1

v2 whole, which is shorter than its diff:
```python
import functools
import math

import jax
import jax.numpy as jnp
import numpy as np
from jax import lax
from jax.experimental import pallas as pl
from jax.experimental.pallas import tpu as pltpu
from jax.sharding import PartitionSpec as P

NBLK = 8
LANES = 128
VMEM = pl.BlockSpec(memory_space=pltpu.VMEM)
SMEM = pl.BlockSpec(memory_space=pltpu.SMEM)
MESH = pl.DeviceIdType.MESH
HIGH = lax.Precision.HIGHEST


def turn_coefficients():
    degree = 5
    nodes = np.cos((np.arange(64) + 0.5) * np.pi / 64) * 0.125 + 0.125
    root = np.sqrt(nodes)
    cos_fit = np.polynomial.Chebyshev.fit(nodes, np.cos(2 * np.pi * root), degree, domain=[0, 0.25])
    sin_fit = np.polynomial.Chebyshev.fit(
        nodes, np.sin(2 * np.pi * root) / root, degree, domain=[0, 0.25]
    )
    as_power = lambda fit: [float(np.float32(v)) for v in fit.convert(kind=np.polynomial.Polynomial).coef]
    return as_power(cos_fit), as_power(sin_fit)


COS_COEF, SIN_COEF = turn_coefficients()


def cos_sin_turns(turns):
    r = turns - jnp.floor(turns + 0.5)
    s = r * r
    c = jnp.full_like(s, COS_COEF[-1])
    q = jnp.full_like(s, SIN_COEF[-1])
    for a, b in zip(COS_COEF[-2::-1], SIN_COEF[-2::-1]):
        c = c * s + a
        q = q * s + b
    return c, q * r


def forward_seeds(samples):
    fine = 32
    quarter = samples // 4
    f = (4 * np.arange(quarter // 4)[None, :] + np.arange(4)[:, None]).reshape(-1)
    coarse = (np.arange(quarter // fine) * fine)[:, None] * f[None, :] % samples
    small = np.arange(fine)[:, None] * f[None, :] % samples
    out = []
    for product in (coarse, small):
        angle = product * (2 * np.pi / samples)
        out += [np.cos(angle), np.sin(angle)]
    return [v.astype(np.float32) for v in out]


def inverse_seeds(samples, channels):
    halves = samples // 16 // LANES
    lane = np.arange(LANES)
    r = np.repeat(np.arange(4), halves)
    h = np.tile(np.arange(halves), 4)
    f = 4 * LANES * h[:, None] + 4 * lane[None, :] + r[:, None]
    weight = np.where(f == 0, 1.0, 2.0) / (samples * math.sqrt(channels))
    angle = (f[:, :, None] * np.arange(LANES)[None, None, :] % samples) * (2 * np.pi / samples)
    first = [weight[:, :, None] * np.cos(angle), weight[:, :, None] * np.sin(angle)]
    steps = samples // LANES
    b = 4 * lane[None, :] + np.arange(4)[:, None]
    turn = (b[:, None, :] * np.arange(steps)[None, :, None] % steps) * (2 * np.pi / steps)
    second = [np.cos(turn), np.sin(turn)]
    return [v.astype(np.float32) for v in first + second]


def member_rows(edges_ref, channel, bands, channels):
    rows = []
    for j in range(bands):
        inside = channel < (channels if j == bands - 1 else edges_ref[j])
        if j:
            inside = jnp.logical_and(inside, channel >= edges_ref[j - 1])
        rows.append(inside)
    return rows


def fused_kernel(
    n, bands, channels, trials,
    edges_ref, delays_ref, mask_ref, x_ref, ac_ref, as_ref, bc_ref, bs_ref,
    out_ref,
    acc_ref, tab_cos, tab_sin, y_ref, spec_re, spec_im, rot_ref, frac_ref,
    own_power, got_power, part_ref, got_part,
    power_send, power_recv, part_send, part_recv,
):
    local, samples = x_ref.shape
    quarter = samples // 4
    window = samples // NBLK
    group = quarter // 4
    halves = group // LANES
    share = out_ref.shape[0]
    fine = bc_ref.shape[0]
    me = lax.axis_index("wide")
    first = me * local

    barrier = pltpu.get_barrier_semaphore()
    for step in range(1, n):
        pl.semaphore_signal(
            barrier, inc=1, device_id={"wide": lax.rem(me + step, n)}, device_id_type=MESH
        )

    rows = 64

    def square(i, carry):
        at = pl.ds(pl.multiple_of(i * rows, rows), rows)
        for k in range(NBLK):
            total = None
            for p in range(window // LANES):
                v = x_ref[at, pl.ds(k * window + p * LANES, LANES)].astype(jnp.float32)
                total = v * v if total is None else total + v * v
            acc_ref[at, pl.ds(k * LANES, LANES)] = total
        return carry

    lax.fori_loop(0, local // rows, square, 0)
    channel_row = first + lax.broadcasted_iota(jnp.int32, (1, local), 1)
    keep = mask_ref[...].astype(jnp.float32)
    picks = [jnp.where(m, keep, 0.0) for m in member_rows(edges_ref, channel_row, bands, channels)]
    pick = jnp.concatenate(picks, axis=0)
    summed = jnp.dot(pick, acc_ref[...], precision=HIGH, preferred_element_type=jnp.float32)
    spot = lax.broadcasted_iota(jnp.int32, (bands, LANES), 1)
    powers = jnp.zeros((bands, LANES), jnp.float32)
    for k in range(NBLK):
        part = jnp.sum(summed[:, k * LANES : (k + 1) * LANES], axis=1, keepdims=True)
        powers = jnp.where(spot == k, part / window, powers)
    own_power[...] = powers

    channel = first + lax.broadcasted_iota(jnp.int32, (local, LANES), 0)
    ratio = 0.5 + 0.5 * (channel.astype(jnp.float32) + 0.5) / channels
    fraction = (1.0 / (ratio * ratio) - 1.0) / 3.0
    frac_ref[...] = fraction
    lane = lax.broadcasted_iota(jnp.int32, (1, LANES), 1)
    delay_row = jnp.zeros((1, LANES), jnp.float32)
    for d in range(trials):
        delay_row = jnp.where(lane == d, delays_ref[d].astype(jnp.float32), delay_row)
    sweep = fraction * (delay_row * (1.0 / samples))
    rotations = cos_sin_turns(sweep) + cos_sin_turns(sweep * (4.0 * LANES))

    pl.semaphore_wait(barrier, n - 1)
    power_copies = []
    for step in range(1, n):
        copy = pltpu.make_async_remote_copy(
            src_ref=own_power,
            dst_ref=got_power.at[step],
            send_sem=power_send.at[step],
            recv_sem=power_recv.at[step],
            device_id={"wide": lax.rem(me + step, n)},
            device_id_type=MESH,
        )
        copy.start()
        power_copies.append(copy)

    for d in range(trials):
        for i, rot in enumerate(rotations):
            rot_ref[d, i] = jnp.broadcast_to(rot[:, d : d + 1], (local, LANES))

    def fill(i, carry):
        at = pl.ds(pl.multiple_of(i * fine, fine), fine)
        ca, sa = ac_ref[pl.ds(i, 1), :], as_ref[pl.ds(i, 1), :]
        cb, sb = bc_ref[...], bs_ref[...]
        tab_cos[at, :] = (ca * cb - sa * sb).astype(jnp.bfloat16)
        tab_sin[at, :] = (sa * cb + ca * sb).astype(jnp.bfloat16)
        return carry

    lax.fori_loop(0, quarter // fine, fill, 0)

    band_power = own_power[...]
    for step in range(1, n):
        power_copies[step - 1].wait()
        band_power = band_power + got_power[step]

    scale = jnp.zeros((local, LANES), jnp.float32)
    members = member_rows(edges_ref, channel, bands, channels)
    for j in range(bands):
        high = channels if j == bands - 1 else edges_ref[j]
        low = edges_ref[j - 1] if j else 0
        width = jnp.full((1, LANES), high - low, jnp.int32).astype(jnp.float32)
        level = 1.0 / jnp.sqrt(band_power[j : j + 1, :] / width + 1e-05)
        scale = jnp.where(members[j], level, scale)
    scale = scale * jnp.transpose(jnp.broadcast_to(keep, (LANES, local)))

    per = quarter // window
    for h in range(per):
        columns = [scale[:, m * per + h : m * per + h + 1] for m in range(4)]
        for p in range(window // LANES):
            start = h * window + p * LANES
            x0, x1, x2, x3 = (
                x_ref[:, m * quarter + start : m * quarter + start + LANES].astype(jnp.float32)
                * columns[m]
                for m in range(4)
            )
            here = slice(start, start + LANES)
            y_ref[0, :, here] = ((x0 + x2) + (x1 + x3)).astype(jnp.bfloat16)
            y_ref[1, :, here] = ((x0 + x2) - (x1 + x3)).astype(jnp.bfloat16)
            y_ref[2, :, here] = (x0 - x2).astype(jnp.bfloat16)
            y_ref[3, :, here] = (x1 - x3).astype(jnp.bfloat16)

    def product(which, table, r):
        return jnp.dot(
            y_ref[which], table[:, r * group : (r + 1) * group], preferred_element_type=jnp.float32
        )

    def put(r, real, imag):
        spec_re[:, r * group : (r + 1) * group] = real
        spec_im[:, r * group : (r + 1) * group] = imag

    put(0, product(0, tab_cos, 0), -product(0, tab_sin, 0))
    put(2, product(1, tab_cos, 2), -product(1, tab_sin, 2))
    put(1, product(2, tab_cos, 1) - product(3, tab_sin, 1),
        -(product(2, tab_sin, 1) + product(3, tab_cos, 1)))
    put(3, product(2, tab_cos, 3) + product(3, tab_sin, 3),
        product(3, tab_cos, 3) - product(2, tab_sin, 3))

    lane_step = lax.broadcasted_iota(jnp.int32, (8, LANES), 1).astype(jnp.float32) * 4.0
    blocks = 4 * halves
    early = max(1, local // 32)

    def part_copy(step):
        return pltpu.make_async_remote_copy(
            src_ref=part_ref.at[step],
            dst_ref=got_part.at[step],
            send_sem=part_send.at[step],
            recv_sem=part_recv.at[step],
            device_id={"wide": lax.rem(me + step, n)},
            device_id_type=MESH,
        )

    def owner_step(step, carry):
        owner = lax.rem(me + step, n)
        for sub in range(share):
            d = owner * share + sub
            delay = delays_ref[d].astype(jnp.float32) * (1.0 / samples)
            per_lane = lane_step * delay

            def rotate(i, totals):
                at = pl.ds(pl.multiple_of(i * 8, 8), 8)
                base_re, base_im = cos_sin_turns(frac_ref[at, :] * per_lane)
                one_re, one_im = rot_ref[d, 0, at, :], rot_ref[d, 1, at, :]
                far_re, far_im = rot_ref[d, 2, at, :], rot_ref[d, 3, at, :]
                twice = one_re + one_re
                totals = list(totals)
                for h in range(halves):
                    phases = [
                        (base_re, base_im),
                        (base_re * one_re - base_im * one_im, base_re * one_im + base_im * one_re),
                    ]
                    for r in range(4):
                        if r > 1:
                            (b_re, b_im), (a_re, a_im) = phases[-2:]
                            phases.append((twice * a_re - b_re, twice * a_im - b_im))
                        e_re, e_im = phases[r]
                        k = r * halves + h
                        col = pl.ds(k * LANES, LANES)
                        s_re, s_im = spec_re[at, col], spec_im[at, col]
                        totals[k] = totals[k] + (s_re * e_re - s_im * e_im)
                        totals[blocks + k] = totals[blocks + k] + (s_re * e_im + s_im * e_re)
                    if h < halves - 1:
                        base_re, base_im = (
                            base_re * far_re - base_im * far_im,
                            base_re * far_im + base_im * far_re,
                        )
                return tuple(totals)

            zero = jnp.zeros((8, LANES), jnp.float32)
            totals = lax.fori_loop(0, early, rotate, (zero,) * (2 * blocks))
            if sub == 0:

                @pl.when(step > 1)
                def _():
                    part_copy(step - 1).start()

            totals = lax.fori_loop(early, local // 8, rotate, totals)
            part_ref[step, sub] = jnp.concatenate(
                [jnp.sum(v, axis=0, keepdims=True) for v in totals], axis=0
            )
        return carry

    lax.fori_loop(1, n + 1, owner_step, 0)
    total = part_ref[n]
    for step in range(1, n):
        part_copy(step).wait()
        total = total + got_part[step]
    out_ref[...] = total


def series_kernel(x_ref, fc_ref, fs_ref, gc_ref, gs_ref, out_ref):
    blocks = fc_ref.shape[0]
    halves = blocks // 4
    for b in range(x_ref.shape[0]):
        rounded = x_ref[b].astype(jnp.bfloat16).astype(jnp.float32)
        turned = jnp.transpose(rounded)
        series = None
        for r in range(4):
            re = im = None
            for h in range(halves):
                k = r * halves + h
                d_re, d_im = turned[:, k : k + 1], turned[:, blocks + k : blocks + k + 1]
                p_re = d_re * fc_ref[k] - d_im * fs_ref[k]
                p_im = d_re * fs_ref[k] + d_im * fc_ref[k]
                re = p_re if re is None else re + p_re
                im = p_im if im is None else im + p_im
            part = jnp.dot(
                gc_ref[r], re, precision=HIGH, preferred_element_type=jnp.float32
            ) - jnp.dot(gs_ref[r], im, precision=HIGH, preferred_element_type=jnp.float32)
            series = part if series is None else series + part
        out_ref[b] = series


def body(n, filterbank, channel_mask, band_edges, dm_delays):
    beams, local, samples = filterbank.shape
    channels = local * n
    bands = band_edges.shape[0] + 1
    trials = dm_delays.shape[0]
    share = trials // n
    quarter = samples // 4
    blocks = quarter // LANES
    steps = samples // LANES
    ac, as_, bc, bs = forward_seeds(samples)
    fc, fs, gc, gs = inverse_seeds(samples, channels)
    x = filterbank.reshape(local, samples)

    slot = (share, 2 * blocks, LANES)
    dma = pltpu.SemaphoreType.DMA((n,))
    summed = pl.pallas_call(
        functools.partial(fused_kernel, n, bands, channels, trials),
        out_shape=jax.ShapeDtypeStruct(slot, jnp.float32),
        in_specs=[SMEM, SMEM] + [VMEM] * 6,
        out_specs=VMEM,
        scratch_shapes=[
            pltpu.VMEM((local, NBLK * LANES), jnp.float32),
            pltpu.VMEM((quarter, quarter), jnp.bfloat16),
            pltpu.VMEM((quarter, quarter), jnp.bfloat16),
            pltpu.VMEM((4, local, quarter), jnp.bfloat16),
            pltpu.VMEM((local, quarter), jnp.float32),
            pltpu.VMEM((local, quarter), jnp.float32),
            pltpu.VMEM((trials, 4, local, LANES), jnp.float32),
            pltpu.VMEM((local, LANES), jnp.float32),
            pltpu.VMEM((bands, LANES), jnp.float32),
            pltpu.VMEM((n, bands, LANES), jnp.float32),
            pltpu.VMEM((n + 1,) + slot, jnp.float32),
            pltpu.VMEM((n,) + slot, jnp.float32),
            dma, dma, dma, dma,
        ],
        compiler_params=pltpu.CompilerParams(collective_id=0, has_side_effects=True),
    )(band_edges, dm_delays, channel_mask.reshape(1, local), x, ac, as_, bc, bs)
    series = pl.pallas_call(
        series_kernel,
        out_shape=jax.ShapeDtypeStruct((share, steps, LANES), jnp.float32),
        in_specs=[VMEM] * 5,
        out_specs=VMEM,
    )(summed, fc, fs, gc, gs)
    return series.reshape(beams, share, samples)


def solution(mesh):
    return jax.shard_map(
        functools.partial(body, mesh.shape["wide"]),
        mesh=mesh,
        in_specs=(P("beam", "wide", None), P(("beam", "wide")), P(), P()),
        out_specs=P("beam", "wide", None),
        check_vma=False,
    )
```

time: 54.6 us -> 37.7 us (0.69)
  Pallas kernels: 53.5 us -> 37.2 us
  local copies, waits for them, and re-layouts: 0.8 us -> 0 us
    pallas_call x4 -> x1, Pallas kernels: 50.9 us -> 34.6 us  [body(): pl.pallas_call(functools.partial(fused_kernel, n, bands, channels, trials...]
    reshape x1 -> x0, local copies, waits for them, and re-layouts: 0.8 us -> none  [body(): channel_mask.reshape(local, 1)]
where the time goes in v2:
time: 37.7 us; the launch traced here: 37.2 us
  Pallas kernels  37.2 us (99%)
    pallas_call x1, Pallas kernels, body(): pl.pallas_call(functools.partial(fused_kernel, n, bands, channels, trials...  34.6 us
    pallas_call x1, Pallas kernels, body(): pl.pallas_call(series_kernel, out_shape=jax.ShapeDtypeStruct((share, step...  2.61 us

profile of v2, /device:TPU:0, one launch (start us, length us, event | category | flops | bytes accessed | tf_op | source)
XLA Modules:
  0.0 37.2 jit_solution(6664062166889386558)
XLA Ops:
  0.0 34.6 %shard_map.118.x_ref = f32[1,16,128]{2,1,0:T(8,128)} custom-call(s32[7]{0:T(128)} %edges_ref.1, s32[16]{0:T(128)} %delays_ref.1, s32[1,256]{1,0:T(1,128)} %bitcast.4, bf16[256,4096]{1,0:T(8,128)(2,1)} %bitcast.3, f32[32,1024]{1,0:T(8,128)} %constant.16.clone.ac_ref, f32[32,1024]{1,0:T(8,128)} %constant.17.clone.as_ref, f32[32,1024]{1,0:T(8,128)} %constant.18.clone.bc_ref, ...), custom_call_target="tpu_custom_call" | custom-call | tf_op jit(solution)/shard_map/pallas_call | solution.py:330
  34.6 2.6 %shard_map.119 = f32[1,32,128]{2,1,0:T(8,128)} custom-call(f32[1,16,128]{2,1,0:T(8,128)} %shard_map.118.x_ref, f32[8,128,128]{2,1,0:T(8,128)} %constant.20.clone.fc_ref, f32[8,128,128]{2,1,0:T(8,128)} %constant.21.clone.fs_ref, f32[4,32,128]{2,1,0:T(8,128)} %constant.22.clone.gc_ref, f32[4,32,128]{2,1,0:T(8,128)} %constant.23.clone.gs_ref), custom_call_target="tpu_custom_call" | custom-call | tf_op jit(solution)/shard_map/pallas_call | solution.py:352

commit v3 on v2

--- a/solution.py
+++ b/solution.py
@@ -268,14 +268,14 @@
                 return tuple(totals)
 
             zero = jnp.zeros((8, LANES), jnp.float32)
-            totals = lax.fori_loop(0, early, rotate, (zero,) * (2 * blocks))
+            totals = lax.fori_loop(0, early, rotate, (zero,) * (2 * blocks), unroll=4)
             if sub == 0:
 
                 @pl.when(step > 1)
                 def _():
                     part_copy(step - 1).start()
 
-            totals = lax.fori_loop(early, local // 8, rotate, totals)
+            totals = lax.fori_loop(early, local // 8, rotate, totals, unroll=4)
             part_ref[step, sub] = jnp.concatenate(
                 [jnp.sum(v, axis=0, keepdims=True) for v in totals], axis=0
             )

time: 37.7 us -> 29.9 us (0.79)
  Pallas kernels: 37.2 us -> 29.7 us
    pallas_call x1, Pallas kernels: 34.6 us -> 27.1 us  [body(): pl.pallas_call(functools.partial(fused_kernel, n, bands, channels, trials...]
where the time goes in v3:
time: 29.9 us; the launch traced here: 29.7 us
  Pallas kernels  29.7 us (99%)
    pallas_call x1, Pallas kernels, body(): pl.pallas_call(functools.partial(fused_kernel, n, bands, channels, trials...  27.1 us
    pallas_call x1, Pallas kernels, body(): pl.pallas_call(series_kernel, out_shape=jax.ShapeDtypeStruct((share, step...  2.61 us

profile of v3, /device:TPU:0, one launch (start us, length us, event | category | flops | bytes accessed | tf_op | source)
XLA Modules:
  0.0 29.7 jit_solution(6817758635031112397)
XLA Ops:
  0.0 27.1 %shard_map.118.x_ref = f32[1,16,128]{2,1,0:T(8,128)} custom-call(s32[7]{0:T(128)} %edges_ref.1, s32[16]{0:T(128)} %delays_ref.1, s32[1,256]{1,0:T(1,128)} %bitcast.4, bf16[256,4096]{1,0:T(8,128)(2,1)} %bitcast.3, f32[32,1024]{1,0:T(8,128)} %constant.16.clone.ac_ref, f32[32,1024]{1,0:T(8,128)} %constant.17.clone.as_ref, f32[32,1024]{1,0:T(8,128)} %constant.18.clone.bc_ref, ...), custom_call_target="tpu_custom_call" | custom-call | tf_op jit(solution)/shard_map/pallas_call | solution.py:330
  27.1 2.6 %shard_map.119 = f32[1,32,128]{2,1,0:T(8,128)} custom-call(f32[1,16,128]{2,1,0:T(8,128)} %shard_map.118.x_ref, f32[8,128,128]{2,1,0:T(8,128)} %constant.20.clone.fc_ref, f32[8,128,128]{2,1,0:T(8,128)} %constant.21.clone.fs_ref, f32[4,32,128]{2,1,0:T(8,128)} %constant.22.clone.gc_ref, f32[4,32,128]{2,1,0:T(8,128)} %constant.23.clone.gs_ref), custom_call_target="tpu_custom_call" | custom-call | tf_op jit(solution)/shard_map/pallas_call | solution.py:352

commit v4 on v3

--- a/solution.py
+++ b/solution.py
@@ -68,8 +68,9 @@
     steps = samples // LANES
     b = 4 * lane[None, :] + np.arange(4)[:, None]
     turn = (b[:, None, :] * np.arange(steps)[None, :, None] % steps) * (2 * np.pi / steps)
-    second = [np.cos(turn), np.sin(turn)]
-    return [v.astype(np.float32) for v in first + second]
+    second = np.stack([np.cos(turn), -np.sin(turn)], axis=1).reshape(8, steps, LANES)
+    second = np.concatenate(list(second), axis=1)
+    return [v.astype(np.float32) for v in first + [second]]
 
 
 def member_rows(edges_ref, channel, bands, channels):
@@ -82,13 +83,23 @@
     return rows
 
 
+def partner(me, step, n):
+    if n & (n - 1):
+        return lax.rem(me + step, n)
+    out, bit = 0, 1
+    while bit < n:
+        out = out + lax.rem(me // bit + step // bit, 2) * bit
+        bit *= 2
+    return out
+
+
 def fused_kernel(
     n, bands, channels, trials,
-    edges_ref, delays_ref, mask_ref, x_ref, ac_ref, as_ref, bc_ref, bs_ref,
+    edges_ref, delays_ref, mask_ref, x_hbm, ac_ref, as_ref, bc_ref, bs_ref,
     out_ref,
-    acc_ref, tab_cos, tab_sin, y_ref, spec_re, spec_im, rot_ref, frac_ref,
+    x_ref, acc_ref, tab_cos, tab_sin, y_ref, spec_re, spec_im, rot_ref, base_ref, frac_ref,
     own_power, got_power, part_ref, got_part,
-    power_send, power_recv, part_send, part_recv,
+    x_sem, power_send, power_recv, part_send, part_recv,
 ):
     local, samples = x_ref.shape
     quarter = samples // 4
@@ -108,7 +119,25 @@
 
     rows = 64
 
+    def load(i):
+        at = pl.ds(pl.multiple_of(i * rows, rows), rows)
+        return pltpu.make_async_copy(x_hbm.at[at], x_ref.at[at], x_sem.at[i])
+
+    for i in range(local // rows):
+        load(i).start()
+
+    def fill(i, carry):
+        at = pl.ds(pl.multiple_of(i * fine, fine), fine)
+        ca, sa = ac_ref[pl.ds(i, 1), :], as_ref[pl.ds(i, 1), :]
+        cb, sb = bc_ref[...], bs_ref[...]
+        tab_cos[at, :] = (ca * cb - sa * sb).astype(jnp.bfloat16)
+        tab_sin[at, :] = (sa * cb + ca * sb).astype(jnp.bfloat16)
+        return carry
+
+    lax.fori_loop(0, quarter // fine, fill, 0)
+
     def square(i, carry):
+        load(i).wait()
         at = pl.ds(pl.multiple_of(i * rows, rows), rows)
         for k in range(NBLK):
             total = None
@@ -160,15 +189,19 @@
         for i, rot in enumerate(rotations):
             rot_ref[d, i] = jnp.broadcast_to(rot[:, d : d + 1], (local, LANES))
 
-    def fill(i, carry):
-        at = pl.ds(pl.multiple_of(i * fine, fine), fine)
-        ca, sa = ac_ref[pl.ds(i, 1), :], as_ref[pl.ds(i, 1), :]
-        cb, sb = bc_ref[...], bs_ref[...]
-        tab_cos[at, :] = (ca * cb - sa * sb).astype(jnp.bfloat16)
-        tab_sin[at, :] = (sa * cb + ca * sb).astype(jnp.bfloat16)
-        return carry
-
-    lax.fori_loop(0, quarter // fine, fill, 0)
+    def base(d, carry):
+        delay = delays_ref[d].astype(jnp.float32) * (1.0 / samples)
+        per_lane = lane_step * delay
+
+        def tile(i, inner):
+            at = pl.ds(pl.multiple_of(i * 8, 8), 8)
+            base_ref[d, 0, at, :], base_ref[d, 1, at, :] = cos_sin_turns(frac_ref[at, :] * per_lane)
+            return inner
+
+        return lax.fori_loop(0, local // 8, tile, carry, unroll=8)
+
+    lane_step = lax.broadcasted_iota(jnp.int32, (8, LANES), 1).astype(jnp.float32) * 4.0
+    lax.fori_loop(0, trials, base, 0)
 
     band_power = own_power[...]
     for step in range(1, n):
@@ -217,7 +250,6 @@
     put(3, product(2, tab_cos, 3) + product(3, tab_sin, 3),
         product(3, tab_cos, 3) - product(2, tab_sin, 3))
 
-    lane_step = lax.broadcasted_iota(jnp.int32, (8, LANES), 1).astype(jnp.float32) * 4.0
     blocks = 4 * halves
     early = max(1, local // 32)
 
@@ -227,20 +259,19 @@
             dst_ref=got_part.at[step],
             send_sem=part_send.at[step],
             recv_sem=part_recv.at[step],
-            device_id={"wide": lax.rem(me + step, n)},
+            device_id={"wide": partner(me, step, n)},
             device_id_type=MESH,
         )
 
-    def owner_step(step, carry):
-        owner = lax.rem(me + step, n)
+    def owner_step(turn, carry):
+        step = n - 1 - turn
+        owner = partner(me, step, n)
         for sub in range(share):
             d = owner * share + sub
-            delay = delays_ref[d].astype(jnp.float32) * (1.0 / samples)
-            per_lane = lane_step * delay
 
             def rotate(i, totals):
                 at = pl.ds(pl.multiple_of(i * 8, 8), 8)
-                base_re, base_im = cos_sin_turns(frac_ref[at, :] * per_lane)
+                base_re, base_im = base_ref[d, 0, at, :], base_ref[d, 1, at, :]
                 one_re, one_im = rot_ref[d, 0, at, :], rot_ref[d, 1, at, :]
                 far_re, far_im = rot_ref[d, 2, at, :], rot_ref[d, 3, at, :]
                 twice = one_re + one_re
@@ -271,9 +302,9 @@
             totals = lax.fori_loop(0, early, rotate, (zero,) * (2 * blocks), unroll=4)
             if sub == 0:
 
-                @pl.when(step > 1)
+                @pl.when(turn > 0)
                 def _():
-                    part_copy(step - 1).start()
+                    part_copy(step + 1).start()
 
             totals = lax.fori_loop(early, local // 8, rotate, totals, unroll=4)
             part_ref[step, sub] = jnp.concatenate(
@@ -281,21 +312,21 @@
             )
         return carry
 
-    lax.fori_loop(1, n + 1, owner_step, 0)
-    total = part_ref[n]
-    for step in range(1, n):
+    lax.fori_loop(0, n, owner_step, 0)
+    total = part_ref[0]
+    for step in range(n - 1, 0, -1):
         part_copy(step).wait()
         total = total + got_part[step]
     out_ref[...] = total
 
 
-def series_kernel(x_ref, fc_ref, fs_ref, gc_ref, gs_ref, out_ref):
+def series_kernel(x_ref, fc_ref, fs_ref, g_ref, out_ref):
     blocks = fc_ref.shape[0]
     halves = blocks // 4
     for b in range(x_ref.shape[0]):
         rounded = x_ref[b].astype(jnp.bfloat16).astype(jnp.float32)
         turned = jnp.transpose(rounded)
-        series = None
+        parts = []
         for r in range(4):
             re = im = None
             for h in range(halves):
@@ -305,11 +336,11 @@
                 p_im = d_re * fs_ref[k] + d_im * fc_ref[k]
                 re = p_re if re is None else re + p_re
                 im = p_im if im is None else im + p_im
-            part = jnp.dot(
-                gc_ref[r], re, precision=HIGH, preferred_element_type=jnp.float32
-            ) - jnp.dot(gs_ref[r], im, precision=HIGH, preferred_element_type=jnp.float32)
-            series = part if series is None else series + part
-        out_ref[b] = series
+            parts += [re, im]
+        out_ref[b] = jnp.dot(
+            g_ref[...], jnp.concatenate(parts, axis=0),
+            precision=HIGH, preferred_element_type=jnp.float32,
+        )
 
 
 def body(n, filterbank, channel_mask, band_edges, dm_delays):
@@ -322,7 +353,7 @@
     blocks = quarter // LANES
     steps = samples // LANES
     ac, as_, bc, bs = forward_seeds(samples)
-    fc, fs, gc, gs = inverse_seeds(samples, channels)
+    fc, fs, g = inverse_seeds(samples, channels)
     x = filterbank.reshape(local, samples)
 
     slot = (share, 2 * blocks, LANES)
@@ -330,9 +361,10 @@
     summed = pl.pallas_call(
         functools.partial(fused_kernel, n, bands, channels, trials),
         out_shape=jax.ShapeDtypeStruct(slot, jnp.float32),
-        in_specs=[SMEM, SMEM] + [VMEM] * 6,
+        in_specs=[SMEM, SMEM, VMEM, pl.BlockSpec(memory_space=pl.ANY)] + [VMEM] * 4,
         out_specs=VMEM,
         scratch_shapes=[
+            pltpu.VMEM((local, samples), x.dtype),
             pltpu.VMEM((local, NBLK * LANES), jnp.float32),
             pltpu.VMEM((quarter, quarter), jnp.bfloat16),
             pltpu.VMEM((quarter, quarter), jnp.bfloat16),
@@ -340,21 +372,22 @@
             pltpu.VMEM((local, quarter), jnp.float32),
             pltpu.VMEM((local, quarter), jnp.float32),
             pltpu.VMEM((trials, 4, local, LANES), jnp.float32),
+            pltpu.VMEM((trials, 2, local, LANES), jnp.float32),
             pltpu.VMEM((local, LANES), jnp.float32),
             pltpu.VMEM((bands, LANES), jnp.float32),
             pltpu.VMEM((n, bands, LANES), jnp.float32),
-            pltpu.VMEM((n + 1,) + slot, jnp.float32),
             pltpu.VMEM((n,) + slot, jnp.float32),
-            dma, dma, dma, dma,
+            pltpu.VMEM((n,) + slot, jnp.float32),
+            pltpu.SemaphoreType.DMA((local // 64,)), dma, dma, dma, dma,
         ],
         compiler_params=pltpu.CompilerParams(collective_id=0, has_side_effects=True),
     )(band_edges, dm_delays, channel_mask.reshape(1, local), x, ac, as_, bc, bs)
     series = pl.pallas_call(
         series_kernel,
         out_shape=jax.ShapeDtypeStruct((share, steps, LANES), jnp.float32),
-        in_specs=[VMEM] * 5,
+        in_specs=[VMEM] * 4,
         out_specs=VMEM,
-    )(summed, fc, fs, gc, gs)
+    )(summed, fc, fs, g)
     return series.reshape(beams, share, samples)
 
 

time: 29.9 us -> 28.5 us (0.953)
  Pallas kernels: 29.7 us -> 28.4 us
    pallas_call x1, Pallas kernels: 27.1 us -> 25.9 us  [body(): pl.pallas_call(functools.partial(fused_kernel, n, bands, channels, trials...]
where the time goes in v4:
time: 28.5 us; the launch traced here: 28.4 us
  Pallas kernels  28.4 us (100%)
    pallas_call x1, Pallas kernels, body(): pl.pallas_call(functools.partial(fused_kernel, n, bands, channels, trials...  25.9 us
    pallas_call x1, Pallas kernels, body(): pl.pallas_call(series_kernel, out_shape=jax.ShapeDtypeStruct((share, step...  2.48 us

profile of v4, /device:TPU:0, one launch (start us, length us, event | category | flops | bytes accessed | tf_op | source)
XLA Modules:
  0.0 28.4 jit_solution(13565423095150769415)
XLA Ops:
  0.0 25.9 %shard_map.109.x_ref = f32[1,16,128]{2,1,0:T(8,128)} custom-call(s32[7]{0:T(128)} %edges_ref.1, s32[16]{0:T(128)} %delays_ref.1, s32[1,256]{1,0:T(1,128)} %bitcast.4, bf16[256,4096]{1,0:T(8,128)(2,1)} %bitcast.3, f32[32,1024]{1,0:T(8,128)} %constant.14.clone.ac_ref, f32[32,1024]{1,0:T(8,128)} %constant.15.clone.as_ref, f32[32,1024]{1,0:T(8,128)} %constant.16.clone.bc_ref, ...), custom_call_target="tpu_custom_call" | custom-call | tf_op jit(solution)/shard_map/pallas_call | solution.py:361
  25.9 2.5 %shard_map.110 = f32[1,32,128]{2,1,0:T(8,128)} custom-call(f32[1,16,128]{2,1,0:T(8,128)} %shard_map.109.x_ref, f32[8,128,128]{2,1,0:T(8,128)} %constant.18.clone.fc_ref, f32[8,128,128]{2,1,0:T(8,128)} %constant.19.clone.fs_ref, f32[32,1024]{1,0:T(8,128)} %constant.20.clone.g_ref), custom_call_target="tpu_custom_call" | custom-call | tf_op jit(solution)/shard_map/pallas_call | solution.py:385

commit v5 on v4

--- a/solution.py
+++ b/solution.py
@@ -46,8 +46,8 @@
 def forward_seeds(samples):
     fine = 32
     quarter = samples // 4
-    f = (4 * np.arange(quarter // 4)[None, :] + np.arange(4)[:, None]).reshape(-1)
-    coarse = (np.arange(quarter // fine) * fine)[:, None] * f[None, :] % samples
+    f = (8 * np.arange(quarter // 8)[None, :] + np.arange(8)[:, None]).reshape(-1)
+    coarse = (np.arange(samples // 8 // fine) * fine)[:, None] * f[None, :] % samples
     small = np.arange(fine)[:, None] * f[None, :] % samples
     out = []
     for product in (coarse, small):
@@ -57,18 +57,15 @@
 
 
 def inverse_seeds(samples, channels):
-    halves = samples // 16 // LANES
     lane = np.arange(LANES)
-    r = np.repeat(np.arange(4), halves)
-    h = np.tile(np.arange(halves), 4)
-    f = 4 * LANES * h[:, None] + 4 * lane[None, :] + r[:, None]
+    f = 8 * lane[None, :] + np.arange(8)[:, None]
     weight = np.where(f == 0, 1.0, 2.0) / (samples * math.sqrt(channels))
     angle = (f[:, :, None] * np.arange(LANES)[None, None, :] % samples) * (2 * np.pi / samples)
     first = [weight[:, :, None] * np.cos(angle), weight[:, :, None] * np.sin(angle)]
     steps = samples // LANES
-    b = 4 * lane[None, :] + np.arange(4)[:, None]
+    b = f
     turn = (b[:, None, :] * np.arange(steps)[None, :, None] % steps) * (2 * np.pi / steps)
-    second = np.stack([np.cos(turn), -np.sin(turn)], axis=1).reshape(8, steps, LANES)
+    second = np.stack([np.cos(turn), -np.sin(turn)], axis=1).reshape(16, steps, LANES)
     second = np.concatenate(list(second), axis=1)
     return [v.astype(np.float32) for v in first + [second]]
 
@@ -97,15 +94,16 @@
     n, bands, channels, trials,
     edges_ref, delays_ref, mask_ref, x_hbm, ac_ref, as_ref, bc_ref, bs_ref,
     out_ref,
-    x_ref, acc_ref, tab_cos, tab_sin, y_ref, spec_re, spec_im, rot_ref, base_ref, frac_ref,
+    x_ref, acc_ref, tab_ref, y_ref, spec_re, spec_im, rot_ref, base_ref, frac_ref,
     own_power, got_power, part_ref, got_part,
     x_sem, power_send, power_recv, part_send, part_recv,
 ):
     local, samples = x_ref.shape
     quarter = samples // 4
     window = samples // NBLK
-    group = quarter // 4
-    halves = group // LANES
+    eighth = samples // 8
+    group = quarter // 8
+    assert group == LANES and eighth == window
     share = out_ref.shape[0]
     fine = bc_ref.shape[0]
     me = lax.axis_index("wide")
@@ -130,11 +128,14 @@
         at = pl.ds(pl.multiple_of(i * fine, fine), fine)
         ca, sa = ac_ref[pl.ds(i, 1), :], as_ref[pl.ds(i, 1), :]
         cb, sb = bc_ref[...], bs_ref[...]
-        tab_cos[at, :] = (ca * cb - sa * sb).astype(jnp.bfloat16)
-        tab_sin[at, :] = (sa * cb + ca * sb).astype(jnp.bfloat16)
+        cos_part = (ca * cb - sa * sb).astype(jnp.bfloat16)
+        sin_part = (sa * cb + ca * sb).astype(jnp.bfloat16)
+        for r in range(8):
+            tab_ref[at, 2 * r * group : (2 * r + 1) * group] = cos_part[:, r * group : (r + 1) * group]
+            tab_ref[at, (2 * r + 1) * group : (2 * r + 2) * group] = sin_part[:, r * group : (r + 1) * group]
         return carry
 
-    lax.fori_loop(0, quarter // fine, fill, 0)
+    lax.fori_loop(0, eighth // fine, fill, 0)
 
     def square(i, carry):
         load(i).wait()
@@ -169,7 +170,7 @@
     for d in range(trials):
         delay_row = jnp.where(lane == d, delays_ref[d].astype(jnp.float32), delay_row)
     sweep = fraction * (delay_row * (1.0 / samples))
-    rotations = cos_sin_turns(sweep) + cos_sin_turns(sweep * (4.0 * LANES))
+    rotations = cos_sin_turns(sweep)
 
     pl.semaphore_wait(barrier, n - 1)
     power_copies = []
@@ -200,7 +201,7 @@
 
         return lax.fori_loop(0, local // 8, tile, carry, unroll=8)
 
-    lane_step = lax.broadcasted_iota(jnp.int32, (8, LANES), 1).astype(jnp.float32) * 4.0
+    lane_step = lax.broadcasted_iota(jnp.int32, (8, LANES), 1).astype(jnp.float32) * 8.0
     lax.fori_loop(0, trials, base, 0)
 
     band_power = own_power[...]
@@ -218,39 +219,49 @@
         scale = jnp.where(members[j], level, scale)
     scale = scale * jnp.transpose(jnp.broadcast_to(keep, (LANES, local)))
 
-    per = quarter // window
-    for h in range(per):
-        columns = [scale[:, m * per + h : m * per + h + 1] for m in range(4)]
-        for p in range(window // LANES):
-            start = h * window + p * LANES
-            x0, x1, x2, x3 = (
-                x_ref[:, m * quarter + start : m * quarter + start + LANES].astype(jnp.float32)
-                * columns[m]
-                for m in range(4)
-            )
-            here = slice(start, start + LANES)
-            y_ref[0, :, here] = ((x0 + x2) + (x1 + x3)).astype(jnp.bfloat16)
-            y_ref[1, :, here] = ((x0 + x2) - (x1 + x3)).astype(jnp.bfloat16)
-            y_ref[2, :, here] = (x0 - x2).astype(jnp.bfloat16)
-            y_ref[3, :, here] = (x1 - x3).astype(jnp.bfloat16)
-
-    def product(which, table, r):
-        return jnp.dot(
-            y_ref[which], table[:, r * group : (r + 1) * group], preferred_element_type=jnp.float32
-        )
-
-    def put(r, real, imag):
-        spec_re[:, r * group : (r + 1) * group] = real
-        spec_im[:, r * group : (r + 1) * group] = imag
-
-    put(0, product(0, tab_cos, 0), -product(0, tab_sin, 0))
-    put(2, product(1, tab_cos, 2), -product(1, tab_sin, 2))
-    put(1, product(2, tab_cos, 1) - product(3, tab_sin, 1),
-        -(product(2, tab_sin, 1) + product(3, tab_cos, 1)))
-    put(3, product(2, tab_cos, 3) + product(3, tab_sin, 3),
-        product(3, tab_cos, 3) - product(2, tab_sin, 3))
-
-    blocks = 4 * halves
+    columns = [scale[:, m : m + 1] for m in range(8)]
+    root = math.sqrt(0.5)
+    for p in range(window // LANES):
+        here = slice(p * LANES, (p + 1) * LANES)
+        x = [
+            x_ref[:, m * window + p * LANES : m * window + (p + 1) * LANES].astype(jnp.float32)
+            * columns[m]
+            for m in range(8)
+        ]
+        plus = [x[m] + x[m + 4] for m in range(4)]
+        minus = [x[m] - x[m + 4] for m in range(4)]
+        even, odd = plus[0] + plus[2], plus[1] + plus[3]
+        near, far = root * (minus[1] - minus[3]), root * (minus[1] + minus[3])
+        folded = (
+            even + odd, even - odd,
+            minus[0] + near, -(far + minus[2]),
+            plus[0] - plus[2], plus[3] - plus[1],
+            minus[0] - near, minus[2] - far,
+        )
+        for i, value in enumerate(folded):
+            y_ref[i, :, here] = value.astype(jnp.bfloat16)
+
+    def product(which, r):
+        both = jnp.dot(
+            y_ref[which], tab_ref[:, 2 * r * group : (2 * r + 2) * group],
+            preferred_element_type=jnp.float32,
+        )
+        return both[:, :group], both[:, group:]
+
+    for r in range(8):
+        to = slice(r * group, (r + 1) * group)
+        if r % 4 == 0:
+            c, q = product(r // 4, r)
+            spec_re[:, to], spec_im[:, to] = c, -q
+        else:
+            kind = min(r, 8 - r)
+            (a_c, a_s), (b_c, b_s) = product(2 * kind, r), product(2 * kind + 1, r)
+            if r < 4:
+                spec_re[:, to], spec_im[:, to] = a_c + b_s, b_c - a_s
+            else:
+                spec_re[:, to], spec_im[:, to] = a_c - b_s, -(b_c + a_s)
+
+    blocks = 8
     early = max(1, local // 32)
 
     def part_copy(step):
@@ -273,40 +284,32 @@
                 at = pl.ds(pl.multiple_of(i * 8, 8), 8)
                 base_re, base_im = base_ref[d, 0, at, :], base_ref[d, 1, at, :]
                 one_re, one_im = rot_ref[d, 0, at, :], rot_ref[d, 1, at, :]
-                far_re, far_im = rot_ref[d, 2, at, :], rot_ref[d, 3, at, :]
                 twice = one_re + one_re
                 totals = list(totals)
-                for h in range(halves):
-                    phases = [
-                        (base_re, base_im),
-                        (base_re * one_re - base_im * one_im, base_re * one_im + base_im * one_re),
-                    ]
-                    for r in range(4):
-                        if r > 1:
-                            (b_re, b_im), (a_re, a_im) = phases[-2:]
-                            phases.append((twice * a_re - b_re, twice * a_im - b_im))
-                        e_re, e_im = phases[r]
-                        k = r * halves + h
-                        col = pl.ds(k * LANES, LANES)
-                        s_re, s_im = spec_re[at, col], spec_im[at, col]
-                        totals[k] = totals[k] + (s_re * e_re - s_im * e_im)
-                        totals[blocks + k] = totals[blocks + k] + (s_re * e_im + s_im * e_re)
-                    if h < halves - 1:
-                        base_re, base_im = (
-                            base_re * far_re - base_im * far_im,
-                            base_re * far_im + base_im * far_re,
-                        )
+                phases = [
+                    (base_re, base_im),
+                    (base_re * one_re - base_im * one_im, base_re * one_im + base_im * one_re),
+                ]
+                for r in range(8):
+                    if r > 1:
+                        (b_re, b_im), (a_re, a_im) = phases[-2:]
+                        phases.append((twice * a_re - b_re, twice * a_im - b_im))
+                    e_re, e_im = phases[r]
+                    col = pl.ds(r * LANES, LANES)
+                    s_re, s_im = spec_re[at, col], spec_im[at, col]
+                    totals[r] = totals[r] + (s_re * e_re - s_im * e_im)
+                    totals[blocks + r] = totals[blocks + r] + (s_re * e_im + s_im * e_re)
                 return tuple(totals)
 
             zero = jnp.zeros((8, LANES), jnp.float32)
-            totals = lax.fori_loop(0, early, rotate, (zero,) * (2 * blocks), unroll=4)
+            totals = lax.fori_loop(0, early, rotate, (zero,) * (2 * blocks), unroll=8)
             if sub == 0:
 
                 @pl.when(turn > 0)
                 def _():
                     part_copy(step + 1).start()
 
-            totals = lax.fori_loop(early, local // 8, rotate, totals, unroll=4)
+            totals = lax.fori_loop(early, local // 8, rotate, totals, unroll=8)
             part_ref[step, sub] = jnp.concatenate(
                 [jnp.sum(v, axis=0, keepdims=True) for v in totals], axis=0
             )
@@ -322,21 +325,13 @@
 
 def series_kernel(x_ref, fc_ref, fs_ref, g_ref, out_ref):
     blocks = fc_ref.shape[0]
-    halves = blocks // 4
     for b in range(x_ref.shape[0]):
         rounded = x_ref[b].astype(jnp.bfloat16).astype(jnp.float32)
         turned = jnp.transpose(rounded)
         parts = []
-        for r in range(4):
-            re = im = None
-            for h in range(halves):
-                k = r * halves + h
-                d_re, d_im = turned[:, k : k + 1], turned[:, blocks + k : blocks + k + 1]
-                p_re = d_re * fc_ref[k] - d_im * fs_ref[k]
-                p_im = d_re * fs_ref[k] + d_im * fc_ref[k]
-                re = p_re if re is None else re + p_re
-                im = p_im if im is None else im + p_im
-            parts += [re, im]
+        for k in range(blocks):
+            d_re, d_im = turned[:, k : k + 1], turned[:, blocks + k : blocks + k + 1]
+            parts += [d_re * fc_ref[k] - d_im * fs_ref[k], d_re * fs_ref[k] + d_im * fc_ref[k]]
         out_ref[b] = jnp.dot(
             g_ref[...], jnp.concatenate(parts, axis=0),
             precision=HIGH, preferred_element_type=jnp.float32,
@@ -366,12 +361,11 @@
         scratch_shapes=[
             pltpu.VMEM((local, samples), x.dtype),
             pltpu.VMEM((local, NBLK * LANES), jnp.float32),
-            pltpu.VMEM((quarter, quarter), jnp.bfloat16),
-            pltpu.VMEM((quarter, quarter), jnp.bfloat16),
-            pltpu.VMEM((4, local, quarter), jnp.bfloat16),
+            pltpu.VMEM((samples // 8, 2 * quarter), jnp.bfloat16),
+            pltpu.VMEM((8, local, samples // 8), jnp.bfloat16),
             pltpu.VMEM((local, quarter), jnp.float32),
             pltpu.VMEM((local, quarter), jnp.float32),
-            pltpu.VMEM((trials, 4, local, LANES), jnp.float32),
+            pltpu.VMEM((trials, 2, local, LANES), jnp.float32),
             pltpu.VMEM((trials, 2, local, LANES), jnp.float32),
             pltpu.VMEM((local, LANES), jnp.float32),
             pltpu.VMEM((bands, LANES), jnp.float32),

time: 28.5 us -> 26.7 us (0.937)
  Pallas kernels: 28.4 us -> 26.5 us
    pallas_call x1, Pallas kernels: 25.9 us -> 23.8 us  [body(): pl.pallas_call(functools.partial(fused_kernel, n, bands, channels, trials...]
where the time goes in v5:
time: 26.7 us; the launch traced here: 26.5 us
  Pallas kernels  26.5 us (99%)
    pallas_call x1, Pallas kernels, body(): pl.pallas_call(functools.partial(fused_kernel, n, bands, channels, trials...  23.8 us
    pallas_call x1, Pallas kernels, body(): pl.pallas_call(series_kernel, out_shape=jax.ShapeDtypeStruct((share, step...  2.74 us

profile of v5, /device:TPU:0, one launch (start us, length us, event | category | flops | bytes accessed | tf_op | source)
XLA Modules:
  0.0 26.5 jit_solution(6329125013609298249)
XLA Ops:
  0.0 23.8 %shard_map.109.x_ref = f32[1,16,128]{2,1,0:T(8,128)} custom-call(s32[7]{0:T(128)} %edges_ref.1, s32[16]{0:T(128)} %delays_ref.1, s32[1,256]{1,0:T(1,128)} %bitcast.4, bf16[256,4096]{1,0:T(8,128)(2,1)} %bitcast.3, f32[16,1024]{1,0:T(8,128)} %constant.14.clone.ac_ref, f32[16,1024]{1,0:T(8,128)} %constant.15.clone.as_ref, f32[32,1024]{1,0:T(8,128)} %constant.16.clone.bc_ref, ...), custom_call_target="tpu_custom_call" | custom-call | tf_op jit(solution)/shard_map/pallas_call | solution.py:356
  23.8 2.7 %shard_map.110 = f32[1,32,128]{2,1,0:T(8,128)} custom-call(f32[1,16,128]{2,1,0:T(8,128)} %shard_map.109.x_ref, f32[8,128,128]{2,1,0:T(8,128)} %constant.18.clone.fc_ref, f32[8,128,128]{2,1,0:T(8,128)} %constant.19.clone.fs_ref, f32[32,2048]{1,0:T(8,128)} %constant.20.clone.g_ref), custom_call_target="tpu_custom_call" | custom-call | tf_op jit(solution)/shard_map/pallas_call | solution.py:379
